TPU v7x, 32 devices: a whole 2x2x4 slice. The times are simulated.
32 devices in a mesh: fsdp: 16 (over z, x, core), col: 2 (over y).
Axes of the slice: x: 2, y: 2, z: 4, core: 2. Of those that a mesh axis runs over, the one named last changes fastest.
Arguments:
- block_input: bfloat16 [2, 16, 128, 2048], P(None, 'fsdp', 'col'), may hold values from -6 to 6
- doc_lengths: int32 [2, 16, 4], P(None, 'fsdp'), may hold values from 1 to 96, 128 in all within a row
- norm_attn: bfloat16 [2048], P('fsdp'), may hold values from 0.099609375 to 1.8984375
- w_query: bfloat16 [2048, 2048], P('fsdp', 'col'), may hold values from -0.125 to 0.125
- w_key: bfloat16 [2048, 1024], P('fsdp', 'col'), may hold values from -0.125 to 0.125
- w_value: bfloat16 [2048, 1024], P('fsdp', 'col'), may hold values from -0.125 to 0.125
- w_gate_attn: bfloat16 [2048, 2048], P('fsdp', 'col'), may hold values from -0.125 to 0.125
- w_out: bfloat16 [2048, 2048], P('fsdp', 'col'), may hold values from -1 to 1
- gain_query: bfloat16 [128], P('fsdp'), may hold values from 0.099609375 to 1.8984375
- gain_key: bfloat16 [128], P('fsdp'), may hold values from 0.099609375 to 1.8984375
- norm_ffn: bfloat16 [2048], P('fsdp'), may hold values from 0.099609375 to 1.8984375
- w_gate: bfloat16 [2048, 6144], P('fsdp', 'col'), may hold values from -0.125 to 0.125
- w_up: bfloat16 [2048, 6144], P('fsdp', 'col'), may hold values from -0.125 to 0.125
- w_down: bfloat16 [6144, 2048], P('fsdp', 'col'), may hold values from -0.078125 to 0.078125
- grad_output: bfloat16 [2, 16, 128, 2048], P(None, 'fsdp', 'col'), may hold values from -6 to 6
Outputs:
- block_output: bfloat16 [2, 16, 128, 2048], P(None, 'fsdp', 'col')
- grad_input: float32 [2, 16, 128, 2048], P(None, 'fsdp', 'col')
- grad_norm_attn: float32 [2048], P('fsdp')
- grad_query: float32 [2048, 2048], P('fsdp', 'col')
- grad_key: float32 [2048, 1024], P('fsdp', 'col')
- grad_value: float32 [2048, 1024], P('fsdp', 'col')
- grad_gate_attn: float32 [2048, 2048], P('fsdp', 'col')
- grad_out: float32 [2048, 2048], P('fsdp', 'col')
- grad_gain_query: float32 [128], P('fsdp')
- grad_gain_key: float32 [128], P('fsdp')
- grad_norm_ffn: float32 [2048], P('fsdp')
- grad_gate: float32 [2048, 6144], P('fsdp', 'col')
- grad_up: float32 [2048, 6144], P('fsdp', 'col')
- grad_down: float32 [6144, 2048], P('fsdp', 'col')
Inputs may be any that keep to these rules, and one draw needn't show every extreme that they name: `doc_lengths`: each bucket holds 4 documents packed in order from position 0; their lengths sum to 128, and in every bucket the longest has exactly 96 tokens.
All inputs are finite; a program needn't handle non-finite values.
Results may differ from a plain program's by a relative error of at most 0.014.
Values may be sent and summed in bfloat16 or wider, within the bound.
No kernel may reach another device: no remote copies, remote signals or barrier semaphores. Data moves between devices by JAX's collectives and lax.ppermute only.
A program may use at most 448 MiB of HBM per device.

v0:
```python
import math

import jax
import jax.numpy as jnp
from jax import lax
from jax.sharding import PartitionSpec as P

eps_norm = 1e-06
theta_base = 1000000.0
masked_score = -1e30


def passed_along(value, axis, steps):
    count = lax.axis_size(axis)
    first, last = (max(0, -steps), min(count, count - steps))
    return lax.ppermute(value, axis, [(source, source + steps) for source in range(first, last)])


def rms_scale(values):
    return lax.rsqrt(jnp.mean(values * values, axis=-1, keepdims=True) + eps_norm)


def norm_part(values, gain_vec):
    return values * rms_scale(values) * gain_vec


def rotate(values, cosine, sine_table):
    half_size = values.shape[-1] // 2
    turned = jnp.concatenate([-values[..., half_size:], values[..., :half_size]], axis=-1)
    return values * cosine + turned * sine_table


def angle_tables(positions, head_size):
    freq_index = jnp.arange(head_size // 2, dtype=jnp.float32)
    inverse = jnp.exp(freq_index * (-2.0 * math.log(theta_base) / head_size))
    angles = positions.astype(jnp.float32)[..., None] * inverse
    angles = jnp.concatenate([angles, angles], axis=-1)
    return (jnp.cos(angles), jnp.sin(angles))


def doc_layout(length_rows, positions):
    ends_sum = jnp.cumsum(length_rows, axis=-1, dtype=jnp.int32)
    passed = positions[None, :, None] >= ends_sum[:, None, :]
    doc_index = jnp.sum(passed.astype(jnp.int32), axis=-1, dtype=jnp.int32)
    starts = jnp.sum(jnp.where(passed, length_rows[:, None, :], 0), axis=-1, dtype=jnp.int32)
    return (doc_index, positions[None, :] - starts)


def assemble(gathered, fsdp_count, col_count):
    if gathered.ndim == 2:
        piece_size = gathered.shape[1]
        return gathered.reshape(fsdp_count, col_count, piece_size)[:, 0].reshape(
            fsdp_count * piece_size
        )
    block_rows = gathered.shape[1]
    block_cols = gathered.shape[2]
    block_grid = gathered.reshape(fsdp_count, col_count, block_rows, block_cols)
    return block_grid.transpose(0, 2, 1, 3).reshape(fsdp_count * block_rows, col_count * block_cols)


def spread_weight(full_grad, fsdp_count, col_count):
    row_total = full_grad.shape[0]
    col_total = full_grad.shape[1]
    block_grid = full_grad.reshape(
        fsdp_count, row_total // fsdp_count, col_count, col_total // col_count
    )
    return block_grid.transpose(0, 2, 1, 3).reshape(
        fsdp_count * col_count * (row_total // fsdp_count), col_total // col_count
    )


def spread_gain(full_grad, fsdp_count, col_count):
    piece_size = full_grad.shape[0] // fsdp_count
    block_grid = jnp.broadcast_to(
        full_grad.reshape(fsdp_count, 1, piece_size), (fsdp_count, col_count, piece_size)
    )
    return block_grid.reshape(fsdp_count * col_count * piece_size)


def collect_attention(shards, fsdp_count, col_count):
    gathered = (
        lax.all_gather(shards[0][None], ("fsdp", "col"), axis=0, tiled=True),
        lax.all_gather(shards[1][None], ("fsdp", "col"), axis=0, tiled=True),
        lax.all_gather(shards[2][None], ("fsdp", "col"), axis=0, tiled=True),
        lax.all_gather(shards[3][None], ("fsdp", "col"), axis=0, tiled=True),
        lax.all_gather(shards[4][None], ("fsdp", "col"), axis=0, tiled=True),
        lax.all_gather(shards[5][None], ("fsdp", "col"), axis=0, tiled=True),
        lax.all_gather(shards[6][None], ("fsdp", "col"), axis=0, tiled=True),
        lax.all_gather(shards[7][None], ("fsdp", "col"), axis=0, tiled=True),
    )
    return tuple((assemble(member, fsdp_count, col_count) for member in gathered))


def collect_ffn(shards, fsdp_count, col_count):
    gathered = (
        lax.all_gather(shards[0][None], ("fsdp", "col"), axis=0, tiled=True),
        lax.all_gather(shards[1][None], ("fsdp", "col"), axis=0, tiled=True),
        lax.all_gather(shards[2][None], ("fsdp", "col"), axis=0, tiled=True),
        lax.all_gather(shards[3][None], ("fsdp", "col"), axis=0, tiled=True),
    )
    return tuple((assemble(member, fsdp_count, col_count) for member in gathered))


def body(
    block_input,
    doc_lengths,
    norm_attn,
    w_query,
    w_key,
    w_value,
    w_gate_attn,
    w_out,
    gain_query,
    gain_key,
    norm_ffn,
    w_gate,
    w_up,
    w_down,
    grad_output,
):
    fsdp_count = lax.axis_size("fsdp")
    col_count = lax.axis_size("col")
    side_index = lax.axis_index("col")
    micro_count = block_input.shape[0]
    local_rows = block_input.shape[2]
    model_width = block_input.shape[3]
    row_total = micro_count * local_rows
    attn_shards = (norm_attn, w_query, w_key, w_value, w_gate_attn, w_out, gain_query, gain_key)
    ffn_shards = (norm_ffn, w_gate, w_up, w_down)
    attn_set = collect_attention(attn_shards, fsdp_count, col_count)
    gain_one, query_mat, key_mat, value_mat, gate_mat, out_mat, query_gain, key_gain = attn_set
    head_size = query_gain.shape[0]
    head_count = query_mat.shape[1] // head_size
    kv_count = key_mat.shape[1] // head_size
    group_size = head_count // kv_count
    scale_factor = head_size ** (-0.5)
    length_rows = doc_lengths.reshape(micro_count, doc_lengths.shape[2])
    query_pos = side_index * local_rows + jnp.arange(local_rows, dtype=jnp.int32)
    key_pos = side_index * local_rows - local_rows + jnp.arange(2 * local_rows, dtype=jnp.int32)
    query_doc, query_inner = doc_layout(length_rows, query_pos)
    key_doc = doc_layout(length_rows, key_pos)[0]
    allowed = (
        (query_doc[:, :, None] == key_doc[:, None, :])
        & (key_pos[None, None, :] <= query_pos[None, :, None])
        & (key_pos[None, None, :] >= 0)
    )
    cosine, sine_table = angle_tables(query_inner.reshape(row_total), head_size)
    cosine = cosine[:, None, :]
    sine_table = sine_table[:, None, :]

    def prep_heads(raw_heads, gain_vec):
        return rotate(norm_part(raw_heads, gain_vec), cosine, sine_table)

    tokens = block_input.reshape(row_total, model_width).astype(jnp.float32)
    gain_one32 = gain_one.astype(jnp.float32)
    hidden_one = norm_part(tokens, gain_one32).astype(jnp.bfloat16)
    query_raw = jnp.dot(hidden_one, query_mat, preferred_element_type=jnp.float32).reshape(
        row_total, head_count, head_size
    )
    key_raw = jnp.dot(hidden_one, key_mat, preferred_element_type=jnp.float32).reshape(
        row_total, kv_count, head_size
    )
    value_rows = jnp.dot(hidden_one, value_mat, preferred_element_type=jnp.float32).astype(
        jnp.bfloat16
    )
    gate_raw = jnp.dot(hidden_one, gate_mat, preferred_element_type=jnp.float32)
    query_gain32 = query_gain.astype(jnp.float32)
    key_gain32 = key_gain.astype(jnp.float32)
    query_rot = prep_heads(query_raw, query_gain32).astype(jnp.bfloat16)
    key_rot = prep_heads(key_raw, key_gain32).astype(jnp.bfloat16)
    key_local = key_rot.reshape(micro_count, local_rows, kv_count, head_size)
    value_local = value_rows.reshape(micro_count, local_rows, kv_count, head_size)
    key_remote, value_remote = passed_along((key_local, value_local), "col", 1)
    key_heads = jnp.concatenate([key_remote, key_local], axis=1).transpose(2, 0, 1, 3)
    value_heads = jnp.concatenate([value_remote, value_local], axis=1).transpose(2, 0, 1, 3)
    query_heads = query_rot.reshape(
        micro_count, local_rows, kv_count, group_size, head_size
    ).transpose(2, 0, 1, 3, 4)

    def score_block(query_head, key_head):
        scores = (
            jnp.einsum("mqgd,msd->mgqs", query_head, key_head, preferred_element_type=jnp.float32)
            * scale_factor
        )
        return jnp.where(allowed[:, None], scores, masked_score)

    def attend(operands):
        query_head, key_head, value_head = operands
        scores = score_block(query_head, key_head)
        row_peak = jnp.max(scores, axis=-1, keepdims=True)
        log_total = row_peak + jnp.log(jnp.sum(jnp.exp(scores - row_peak), axis=-1, keepdims=True))
        prob_rows = jnp.exp(scores - log_total).astype(jnp.bfloat16)
        mixed_head = jnp.einsum(
            "mgqs,msd->mqgd", prob_rows, value_head, preferred_element_type=jnp.float32
        )
        return (mixed_head, log_total)

    mixed_heads, log_totals = lax.map(attend, (query_heads, key_heads, value_heads))
    mixed_rows = mixed_heads.transpose(1, 2, 0, 3, 4).reshape(row_total, head_count * head_size)
    gate_sig = jax.nn.sigmoid(gate_raw)
    gated_rows = (mixed_rows * gate_sig).astype(jnp.bfloat16)
    residual = tokens + jnp.dot(gated_rows, out_mat, preferred_element_type=jnp.float32)
    ffn_set = collect_ffn(ffn_shards, fsdp_count, col_count)
    gain_two, gate_wide, up_wide, down_wide = ffn_set
    gain_two32 = gain_two.astype(jnp.float32)
    hidden_two = norm_part(residual, gain_two32).astype(jnp.bfloat16)
    gate_pre = jnp.dot(hidden_two, gate_wide, preferred_element_type=jnp.float32)
    up_pre = jnp.dot(hidden_two, up_wide, preferred_element_type=jnp.float32)
    inner_act = (jax.nn.silu(gate_pre) * up_pre).astype(jnp.bfloat16)
    final_rows = residual + jnp.dot(inner_act, down_wide, preferred_element_type=jnp.float32)
    block_output = final_rows.astype(jnp.bfloat16).reshape(block_input.shape)
    held_shards = lax.optimization_barrier((ffn_shards, block_output))[0]
    back_ffn = collect_ffn(held_shards, fsdp_count, col_count)
    gate_back = back_ffn[1]
    up_back = back_ffn[2]
    down_back = back_ffn[3]
    cotangent = grad_output.reshape(row_total, model_width)
    cot_wide = cotangent.astype(jnp.float32)
    grad_down_full = jnp.einsum(
        "nf,nd->fd", inner_act, cotangent, preferred_element_type=jnp.float32
    )
    grad_inner = jnp.einsum("nd,fd->nf", cotangent, down_back, preferred_element_type=jnp.float32)

    def swiglu(gate_in, up_in):
        return jax.nn.silu(gate_in) * up_in

    unused_value, swiglu_pull = jax.vjp(swiglu, gate_pre, up_pre)
    grad_gate_pre, grad_up_pre = swiglu_pull(grad_inner)
    grad_gate_pre = grad_gate_pre.astype(jnp.bfloat16)
    grad_up_pre = grad_up_pre.astype(jnp.bfloat16)
    grad_gate_full = jnp.einsum(
        "nd,nf->df", hidden_two, grad_gate_pre, preferred_element_type=jnp.float32
    )
    grad_up_full = jnp.einsum(
        "nd,nf->df", hidden_two, grad_up_pre, preferred_element_type=jnp.float32
    )
    grad_hidden_two = jnp.einsum(
        "nf,df->nd", grad_gate_pre, gate_back, preferred_element_type=jnp.float32
    ) + jnp.einsum("nf,df->nd", grad_up_pre, up_back, preferred_element_type=jnp.float32)
    unused_norm, norm_pull = jax.vjp(norm_part, residual, gain_two32)
    grad_resid_norm, grad_gain_two = norm_pull(grad_hidden_two)
    grad_resid = cot_wide + grad_resid_norm
    ffn_grads = (
        lax.psum_scatter(
            spread_gain(grad_gain_two, fsdp_count, col_count),
            ("fsdp", "col"),
            scatter_dimension=0,
            tiled=True,
        ),
        lax.psum_scatter(
            spread_weight(grad_gate_full, fsdp_count, col_count),
            ("fsdp", "col"),
            scatter_dimension=0,
            tiled=True,
        ),
        lax.psum_scatter(
            spread_weight(grad_up_full, fsdp_count, col_count),
            ("fsdp", "col"),
            scatter_dimension=0,
            tiled=True,
        ),
        lax.psum_scatter(
            spread_weight(grad_down_full, fsdp_count, col_count),
            ("fsdp", "col"),
            scatter_dimension=0,
            tiled=True,
        ),
    )
    held_attn = lax.optimization_barrier((attn_shards, grad_resid))[0]
    back_attn = collect_attention(held_attn, fsdp_count, col_count)
    query_back = back_attn[1]
    key_back = back_attn[2]
    value_back = back_attn[3]
    gate_back_attn = back_attn[4]
    out_back = back_attn[5]
    grad_attn_low = grad_resid.astype(jnp.bfloat16)
    grad_out_full = jnp.einsum(
        "nh,nd->hd", gated_rows, grad_attn_low, preferred_element_type=jnp.float32
    )
    grad_gated = jnp.einsum(
        "nd,hd->nh", grad_attn_low, out_back, preferred_element_type=jnp.float32
    )
    grad_mixed = (grad_gated * gate_sig).astype(jnp.bfloat16)
    grad_gate_raw = (grad_gated * mixed_rows * gate_sig * (1.0 - gate_sig)).astype(jnp.bfloat16)
    grad_mixed_heads = grad_mixed.reshape(
        micro_count, local_rows, kv_count, group_size, head_size
    ).transpose(2, 0, 1, 3, 4)

    def attend_back(operands):
        query_head, key_head, value_head, log_total, grad_head = operands
        scores = score_block(query_head, key_head)
        prob_wide = jnp.exp(scores - log_total)
        prob_rows = prob_wide.astype(jnp.bfloat16)
        grad_probs = jnp.einsum(
            "mqgd,msd->mgqs", grad_head, value_head, preferred_element_type=jnp.float32
        )
        centre = jnp.sum(prob_wide * grad_probs, axis=-1, keepdims=True)
        grad_scores = (prob_wide * (grad_probs - centre)).astype(jnp.bfloat16)
        grad_query_head = (
            jnp.einsum("mgqs,msd->mqgd", grad_scores, key_head, preferred_element_type=jnp.float32)
            * scale_factor
        )
        grad_key_head = (
            jnp.einsum(
                "mgqs,mqgd->msd", grad_scores, query_head, preferred_element_type=jnp.float32
            )
            * scale_factor
        )
        grad_value_head = jnp.einsum(
            "mgqs,mqgd->msd", prob_rows, grad_head, preferred_element_type=jnp.float32
        )
        return (grad_query_head, grad_key_head, grad_value_head)

    grad_query_heads, grad_key_heads, grad_value_heads = lax.map(
        attend_back, (query_heads, key_heads, value_heads, log_totals, grad_mixed_heads)
    )
    key_back_remote, value_back_remote = (
        passed_along(grad_key_heads[:, :, :local_rows].astype(jnp.bfloat16), "col", -1).astype(
            jnp.float32
        ),
        passed_along(grad_value_heads[:, :, :local_rows].astype(jnp.bfloat16), "col", -1).astype(
            jnp.float32
        ),
    )
    grad_key_local = (
        (grad_key_heads[:, :, local_rows:] + key_back_remote)
        .transpose(1, 2, 0, 3)
        .reshape(row_total, kv_count, head_size)
    )
    grad_value_rows = (
        (grad_value_heads[:, :, local_rows:] + value_back_remote)
        .transpose(1, 2, 0, 3)
        .reshape(row_total, kv_count * head_size)
        .astype(jnp.bfloat16)
    )
    grad_query_rot = grad_query_heads.transpose(1, 2, 0, 3, 4).reshape(
        row_total, head_count, head_size
    )
    unused_query, query_pull = jax.vjp(prep_heads, query_raw, query_gain32)
    grad_query_raw, grad_query_gain = query_pull(grad_query_rot)
    unused_key, key_pull = jax.vjp(prep_heads, key_raw, key_gain32)
    grad_key_raw, grad_key_gain = key_pull(grad_key_local)
    grad_query_raw = grad_query_raw.reshape(row_total, head_count * head_size).astype(jnp.bfloat16)
    grad_key_raw = grad_key_raw.reshape(row_total, kv_count * head_size).astype(jnp.bfloat16)
    grad_query_full = jnp.einsum(
        "nd,nh->dh", hidden_one, grad_query_raw, preferred_element_type=jnp.float32
    )
    grad_key_full = jnp.einsum(
        "nd,nh->dh", hidden_one, grad_key_raw, preferred_element_type=jnp.float32
    )
    grad_value_full = jnp.einsum(
        "nd,nh->dh", hidden_one, grad_value_rows, preferred_element_type=jnp.float32
    )
    grad_gate_attn_full = jnp.einsum(
        "nd,nh->dh", hidden_one, grad_gate_raw, preferred_element_type=jnp.float32
    )
    grad_hidden_one = (
        jnp.einsum("nh,dh->nd", grad_query_raw, query_back, preferred_element_type=jnp.float32)
        + jnp.einsum("nh,dh->nd", grad_key_raw, key_back, preferred_element_type=jnp.float32)
        + jnp.einsum("nh,dh->nd", grad_value_rows, value_back, preferred_element_type=jnp.float32)
        + jnp.einsum("nh,dh->nd", grad_gate_raw, gate_back_attn, preferred_element_type=jnp.float32)
    )
    unused_first, first_pull = jax.vjp(norm_part, tokens, gain_one32)
    grad_tokens_norm, grad_gain_one = first_pull(grad_hidden_one)
    grad_input = (grad_resid + grad_tokens_norm).reshape(block_input.shape)
    attn_grads = (
        lax.psum_scatter(
            spread_gain(grad_gain_one, fsdp_count, col_count),
            ("fsdp", "col"),
            scatter_dimension=0,
            tiled=True,
        ),
        lax.psum_scatter(
            spread_gain(grad_query_gain, fsdp_count, col_count),
            ("fsdp", "col"),
            scatter_dimension=0,
            tiled=True,
        ),
        lax.psum_scatter(
            spread_gain(grad_key_gain, fsdp_count, col_count),
            ("fsdp", "col"),
            scatter_dimension=0,
            tiled=True,
        ),
        lax.psum_scatter(
            spread_weight(grad_query_full, fsdp_count, col_count),
            ("fsdp", "col"),
            scatter_dimension=0,
            tiled=True,
        ),
        lax.psum_scatter(
            spread_weight(grad_key_full, fsdp_count, col_count),
            ("fsdp", "col"),
            scatter_dimension=0,
            tiled=True,
        ),
        lax.psum_scatter(
            spread_weight(grad_value_full, fsdp_count, col_count),
            ("fsdp", "col"),
            scatter_dimension=0,
            tiled=True,
        ),
        lax.psum_scatter(
            spread_weight(grad_gate_attn_full, fsdp_count, col_count),
            ("fsdp", "col"),
            scatter_dimension=0,
            tiled=True,
        ),
        lax.psum_scatter(
            spread_weight(grad_out_full, fsdp_count, col_count),
            ("fsdp", "col"),
            scatter_dimension=0,
            tiled=True,
        ),
    )
    return (
        block_output,
        grad_input,
        attn_grads[0],
        attn_grads[3],
        attn_grads[4],
        attn_grads[5],
        attn_grads[6],
        attn_grads[7],
        attn_grads[1],
        attn_grads[2],
        ffn_grads[0],
        ffn_grads[1],
        ffn_grads[2],
        ffn_grads[3],
    )


def solution(mesh):
    in_specs = (
        P(None, "fsdp", "col", None),
        P(None, "fsdp", None),
        P("fsdp"),
        P("fsdp", "col"),
        P("fsdp", "col"),
        P("fsdp", "col"),
        P("fsdp", "col"),
        P("fsdp", "col"),
        P("fsdp"),
        P("fsdp"),
        P("fsdp"),
        P("fsdp", "col"),
        P("fsdp", "col"),
        P("fsdp", "col"),
        P(None, "fsdp", "col", None),
    )
    out_specs = (
        P(None, "fsdp", "col", None),
        P(None, "fsdp", "col", None),
        P("fsdp"),
        P("fsdp", "col"),
        P("fsdp", "col"),
        P("fsdp", "col"),
        P("fsdp", "col"),
        P("fsdp", "col"),
        P("fsdp"),
        P("fsdp"),
        P("fsdp"),
        P("fsdp", "col"),
        P("fsdp", "col"),
        P("fsdp", "col"),
    )
    return jax.shard_map(body, mesh=mesh, in_specs=in_specs, out_specs=out_specs, check_vma=False)
```

profile of v0, /device:TPU:0, one launch (start us, length us, event | category | flops | bytes accessed | tf_op | source)
XLA Modules:
  0.0 4548.1 jit_solution(13921190728572217554)
XLA Ops:
  14.0 70.1 %all-gather.20 = bf16[32,1,128]{2,1,0:T(2,128)(2,1)S(1)} all-gather(bf16[1,1,128]{2,1,0:T(2,128)(2,1)} %bitcast.595), channel_id=2, replica_groups=mesh['fsdp'=16,'col'=2] {'fsdp','col'}, dimensions={0}, use_global_device_ids=true | all-gather | bytes 8448 | tf_op jit(solution)/shard_map/all_gather | solution.py:82
  85.8 37.2 all-reduce.11
  125.1 66.3 %all-gather.21 = bf16[32,1,128]{2,1,0:T(2,128)(2,1)S(1)} all-gather(bf16[1,1,128]{2,1,0:T(2,128)(2,1)} %bitcast.596), channel_id=10, replica_groups=mesh['fsdp'=16,'col'=2] {'fsdp','col'}, dimensions={0}, use_global_device_ids=true | all-gather | bytes 8448 | tf_op jit(solution)/shard_map/all_gather | solution.py:96
  309.1 66.1 %all-gather.47.cloned.1.call-done = bf16[4096,1024]{1,0:T(8,128)(2,1)} async-done(((bf16[128,1024]{1,0:T(8,128)(2,1)}), bf16[4096,1024]{1,0:T(8,128)(2,1)}) %all-gather.47.cloned.1.call-update) | async-done | bytes 8388624 | tf_op jit(solution)/shard_map/all_gather | solution.py:87
  399.7 131.0 %all-gather.51.cloned.1.call-done = bf16[4096,3072]{1,0:T(8,128)(2,1)} async-done(((bf16[128,3072]{1,0:T(8,128)(2,1)}), bf16[4096,3072]{1,0:T(8,128)(2,1)}) %all-gather.51.cloned.1.call-update) | async-done | bytes 25165840 | tf_op jit(solution)/shard_map/all_gather | solution.py:98
  563.3 122.5 %all-gather.55.cloned.1.call-done = bf16[12288,1024]{1,0:T(8,128)(2,1)} async-done(((bf16[384,1024]{1,0:T(8,128)(2,1)}), bf16[12288,1024]{1,0:T(8,128)(2,1)}) %all-gather.55.cloned.1.call-update) | async-done | bytes 25165840 | tf_op jit(solution)/shard_map/all_gather | solution.py:99
  744.5 96.4 %all-gather.49.cloned.1.call-done = bf16[4096,3072]{1,0:T(8,128)(2,1)} async-done(((bf16[128,3072]{1,0:T(8,128)(2,1)}), bf16[4096,3072]{1,0:T(8,128)(2,1)}) %all-gather.49.cloned.1.call-update) | async-done | bytes 25165840 | tf_op jit(solution)/shard_map/all_gather | solution.py:97
  873.6 122.5 %all-gather.59.cloned.1.call-done = bf16[4096,3072]{1,0:T(8,128)(2,1)} async-done(((bf16[128,3072]{1,0:T(8,128)(2,1)}), bf16[4096,3072]{1,0:T(8,128)(2,1)}) %all-gather.59.cloned.1.call-update) | async-done | bytes 25165840 | tf_op jit(solution)/shard_map/all_gather | solution.py:98
  1028.9 122.2 %all-gather.57.cloned.1.call-done = bf16[4096,3072]{1,0:T(8,128)(2,1)} async-done(((bf16[128,3072]{1,0:T(8,128)(2,1)}), bf16[4096,3072]{1,0:T(8,128)(2,1)}) %all-gather.57.cloned.1.call-update) | async-done | bytes 25165840 | tf_op jit(solution)/shard_map/all_gather | solution.py:97
  1260.5 56.8 %all-gather.67.cloned.1.call-done = bf16[4096,512]{1,0:T(8,128)(2,1)} async-done(((bf16[128,512]{1,0:T(8,128)(2,1)}), bf16[4096,512]{1,0:T(8,128)(2,1)}) %all-gather.67.cloned.1.call-update) | async-done | bytes 4194320 | tf_op jit(solution)/shard_map/all_gather | solution.py:85
  1325.7 54.8 %all-gather.65.cloned.1.call-done = bf16[4096,512]{1,0:T(8,128)(2,1)} async-done(((bf16[128,512]{1,0:T(8,128)(2,1)}), bf16[4096,512]{1,0:T(8,128)(2,1)}) %all-gather.65.cloned.1.call-update) | async-done | bytes 4194320 | tf_op jit(solution)/shard_map/all_gather | solution.py:84
  1388.5 71.0 %all-gather.61.cloned.1.call-done = bf16[4096,1024]{1,0:T(8,128)(2,1)} async-done(((bf16[128,1024]{1,0:T(8,128)(2,1)}), bf16[4096,1024]{1,0:T(8,128)(2,1)}) %all-gather.61.cloned.1.call-update) | async-done | bytes 8388624 | tf_op jit(solution)/shard_map/all_gather | solution.py:87
  1479.1 91.4 %while.29 = (s32[]{:T(128)}, f32[8,2,64,2,128]{4,2,1,3,0:T(8,128)}, f32[8,2,128,128]{3,0,2,1:T(8,128)}, f32[8,2,128,128]{3,2,1,0:T(8,128)}, bf16[8,2,128,128]{3,...) while((s32[]{:T(128)}, f32[8,2,64,2,128]{4,2,1,3,0:T(8,128)}, ...), condition=%wide.region_15.16_spmd.clone, body=%wide.region_13.15_spmd.clone.sunk | while | flops 42352384 | bytes 2410281 | solution.py:314
  1747.9 61.9 %reshape.626 = f32[16,128,2,3072]{3,2,1,0:T(2,128)} reshape(f32[2048,6144]{1,0:T(8,128)} %fusion.162) | data formatting | bytes 100663296 | tf_op jit(solution)/shard_map/reshape | solution.py:64
  1809.8 45.5 copy.191
  1876.8 61.8 %reshape.628 = f32[16,128,2,3072]{3,2,1,0:T(2,128)} reshape(f32[2048,6144]{1,0:T(8,128)} %fusion.163) | data formatting | bytes 100663296 | tf_op jit(solution)/shard_map/reshape | solution.py:64
  1938.6 45.5 %copy.192 = f32[16,2,128,3072]{3,2,1,0:T(8,128)} copy(f32[16,2,128,3072]{3,1,2,0:T(2,128)} %bitcast.503) | data formatting | bytes 100663296 | tf_op jit(solution)/shard_map/transpose | solution.py:67
  2086.8 40.9 all-reduce.10
  2150.1 360.5 %reduce-scatter.17.cloned.1.call-done = f32[128,1024]{1,0:T(8,128)} async-done(((f32[4096,1024]{1,0:T(8,128)}), f32[128,1024]{1,0:T(8,128)}) %reduce-scatter.17.cloned.1.call-update) | async-done | bytes 524304 | tf_op jit(solution)/shard_map/reduce_scatter | solution.py:409
  2510.5 361.3 %reduce-scatter.9.cloned.1.call-done = f32[128,1024]{1,0:T(8,128)} async-done(((f32[4096,1024]{1,0:T(8,128)}), f32[128,1024]{1,0:T(8,128)}) %reduce-scatter.9.cloned.1.call-update) | async-done | bytes 524304 | tf_op jit(solution)/shard_map/reduce_scatter | solution.py:385
  2871.8 361.4 %reduce-scatter.15.cloned.1.call-done = f32[128,1024]{1,0:T(8,128)} async-done(((f32[4096,1024]{1,0:T(8,128)}), f32[128,1024]{1,0:T(8,128)}) %reduce-scatter.15.cloned.1.call-update) | async-done | bytes 524304 | tf_op jit(solution)/shard_map/reduce_scatter | solution.py:403
  3233.3 437.3 %reduce-scatter.19.cloned.1.call-done = f32[128,3072]{1,0:T(8,128)} async-done(((f32[4096,3072]{1,0:T(8,128)}), f32[128,3072]{1,0:T(8,128)}) %reduce-scatter.19.cloned.1.call-update) | async-done | bytes 1572880 | tf_op jit(solution)/shard_map/reduce_scatter | solution.py:250
  3670.6 435.2 %reduce-scatter.21.cloned.1.call-done = f32[128,3072]{1,0:T(8,128)} async-done(((f32[4096,3072]{1,0:T(8,128)}), f32[128,3072]{1,0:T(8,128)}) %reduce-scatter.21.cloned.1.call-update) | async-done | bytes 1572880 | tf_op jit(solution)/shard_map/reduce_scatter | solution.py:256
  4105.8 435.2 %reduce-scatter.23.cloned.1.call-done = f32[384,1024]{1,0:T(8,128)} async-done(((f32[12288,1024]{1,0:T(8,128)}), f32[384,1024]{1,0:T(8,128)}) %reduce-scatter.23.cloned.1.call-update) | async-done | bytes 1572880 | tf_op jit(solution)/shard_map/reduce_scatter | solution.py:262
  (482 shorter events, 884.7 us)
Async XLA Ops:
  7.2 187.8 %all-gather.39.cloned.1.call-start = ((), (), s32[]{:S(2)}) async-start(), calls=%async_computation.16 | async-start | bytes 4325376 | tf_op jit(solution)/shard_map/all_gather | solution.py:85
  7.9 195.1 %all-gather.41.cloned.1.call-start = ((), (), s32[]{:S(2)}) async-start(), calls=%async_computation.17 | async-start | bytes 4325376 | tf_op jit(solution)/shard_map/all_gather | solution.py:84
  8.7 220.6 %all-gather.43.cloned.1.call-start = ((), (), s32[]{:S(2)}) async-start(), calls=%async_computation.18 | async-start | bytes 8650752 | tf_op jit(solution)/shard_map/all_gather | solution.py:83
  9.4 287.1 %all-gather.45.cloned.1.call-start = ((), (), s32[]{:S(2)}) async-start(), calls=%async_computation.19 | async-start | bytes 8650752 | tf_op jit(solution)/shard_map/all_gather | solution.py:86
  10.0 365.2 %all-gather.47.cloned.1.call-start = ((), (), s32[]{:S(2)}) async-start(), calls=%async_computation.20 | async-start | bytes 8650752 | tf_op jit(solution)/shard_map/all_gather | solution.py:87
  10.6 520.1 %all-gather.51.cloned.1.call-start = ((), (), s32[]{:S(2)}) async-start(), calls=%async_computation.22 | async-start | bytes 25952256 | tf_op jit(solution)/shard_map/all_gather | solution.py:98
  11.1 674.7 %all-gather.55.cloned.1.call-start = ((), (), s32[]{:S(2)}) async-start(), calls=%async_computation.24 | async-start | bytes 25952256 | tf_op jit(solution)/shard_map/all_gather | solution.py:99
  11.9 829.1 %all-gather.49.cloned.1.call-start = ((), (), s32[]{:S(2)}) async-start(), calls=%async_computation.21 | async-start | bytes 25952256 | tf_op jit(solution)/shard_map/all_gather | solution.py:97
  12.6 983.5 %all-gather.59.cloned.1.call-start = ((), (), s32[]{:S(2)}) async-start(), calls=%async_computation.26 | async-start | bytes 25952256 | tf_op jit(solution)/shard_map/all_gather | solution.py:98
  13.4 1137.7 %all-gather.57.cloned.1.call-start = ((), (), s32[]{:S(2)}) async-start(), calls=%async_computation.25 | async-start | bytes 25952256 | tf_op jit(solution)/shard_map/all_gather | solution.py:97
  14.0 1303.3 %all-gather.67.cloned.1.call-start = ((), (), s32[]{:S(2)}) async-start(), calls=%async_computation.30 | async-start | bytes 4325376 | tf_op jit(solution)/shard_map/all_gather | solution.py:85
  1257.3 123.3 %all-gather.65.cloned.1.call-start = ((), (), s32[]{:S(2)}) async-start(), calls=%async_computation.29 | async-start | bytes 4325376 | tf_op jit(solution)/shard_map/all_gather | solution.py:84
  1257.8 201.8 %all-gather.61.cloned.1.call-start = ((), (), s32[]{:S(2)}) async-start(), calls=%async_computation.27 | async-start | bytes 8650752 | tf_op jit(solution)/shard_map/all_gather | solution.py:87
  1258.6 315.9 %all-gather.63.cloned.1.call-start = ((), (), s32[]{:S(2)}) async-start(), calls=%async_computation.28 | async-start | bytes 8650752 | tf_op jit(solution)/shard_map/all_gather | solution.py:83
  1259.2 363.4 %all-gather.69.cloned.1.call-start = ((), (), s32[]{:S(2)}) async-start(), calls=%async_computation.31 | async-start | bytes 8650752 | tf_op jit(solution)/shard_map/all_gather | solution.py:86
  1259.7 752.0 %all-gather.53.cloned.1.call-start = ((), (), s32[]{:S(2)}) async-start(), calls=%async_computation.23 | async-start | bytes 25952256 | tf_op jit(solution)/shard_map/all_gather | solution.py:99
  1260.3 872.2 %reduce-scatter.11.cloned.1.call-start = ((), (), s32[]{:S(2)}) async-start(), calls=%async_computation.9 | async-start | bytes 8650752 | tf_op jit(solution)/shard_map/reduce_scatter | solution.py:391
  1657.4 492.7 %reduce-scatter.13.cloned.1.call-start = ((), (), s32[]{:S(2)}) async-start(), calls=%async_computation.10 | async-start | bytes 8650752 | tf_op jit(solution)/shard_map/reduce_scatter | solution.py:397
  1662.1 848.4 %reduce-scatter.17.cloned.1.call-start = ((), (), s32[]{:S(2)}) async-start(), calls=%async_computation.12 | async-start | bytes 17301504 | tf_op jit(solution)/shard_map/reduce_scatter | solution.py:409
  1708.8 1163.0 %reduce-scatter.9.cloned.1.call-start = ((), (), s32[]{:S(2)}) async-start(), calls=%async_computation.8 | async-start | bytes 17301504 | tf_op jit(solution)/shard_map/reduce_scatter | solution.py:385
  1717.1 1516.1 %reduce-scatter.15.cloned.1.call-start = ((), (), s32[]{:S(2)}) async-start(), calls=%async_computation.11 | async-start | bytes 17301504 | tf_op jit(solution)/shard_map/reduce_scatter | solution.py:403
  1726.6 1944.0 %reduce-scatter.19.cloned.1.call-start = ((), (), s32[]{:S(2)}) async-start(), calls=%async_computation.13 | async-start | bytes 51904512 | tf_op jit(solution)/shard_map/reduce_scatter | solution.py:250
  1855.3 2250.5 %reduce-scatter.21.cloned.1.call-start = ((), (), s32[]{:S(2)}) async-start(), calls=%async_computation.14 | async-start | bytes 51904512 | tf_op jit(solution)/shard_map/reduce_scatter | solution.py:256
  1984.1 2556.9 %reduce-scatter.23.cloned.1.call-start = ((), (), s32[]{:S(2)}) async-start(), calls=%async_computation.15 | async-start | bytes 51904512 | tf_op jit(solution)/shard_map/reduce_scatter | solution.py:262
  (79 other events, 4178.1 us)
Sparse Core Ops, SparseCore 0:
  10.9 64.4 all-gather.38
  78.2 60.8 all-gather.40
  142.3 75.4 all-gather.42
  220.7 75.7 all-gather.44
  299.4 75.6 all-gather.46
  377.9 152.6 all-gather.50
  533.5 152.2 all-gather.54
  688.7 152.2 all-gather.48
  843.8 152.2 all-gather.58
  998.8 152.2 all-gather.56
  1257.4 59.8 all-gather.66
  1320.0 60.4 all-gather.64
  1383.7 75.8 all-gather.60
  1462.5 75.7 all-gather.62
  1541.3 81.2 all-gather.68
  1625.3 152.6 all-gather.52
  1780.8 181.5 reduce-scatter.10
  1965.1 184.9 reduce-scatter.12
  2152.9 357.5 reduce-scatter.16
  2513.3 358.5 reduce-scatter.8
  2874.7 358.5 reduce-scatter.14
  3240.3 430.2 reduce-scatter.18
  3677.6 428.1 reduce-scatter.20
  4112.7 428.3 reduce-scatter.22
where the time goes:
time: 4570 us; the launch traced here: 4550 us
  waiting for transfers between devices  3310 us (72%)
  local copies, waits for them, and re-layouts  701 us (15%)
  matrix products  275 us (6%)
  blocking collectives  215 us (5%)
    reduce_scatter x1, waiting for transfers between devices, body(): lax.psum_scatter(spread_weight(grad_gate_full, fsdp_count, col_count), ('...  437 us
    reduce_scatter x1, waiting for transfers between devices, body(): lax.psum_scatter(spread_weight(grad_down_full, fsdp_count, col_count), ('...  435 us
    reduce_scatter x1, waiting for transfers between devices, body(): lax.psum_scatter(spread_weight(grad_up_full, fsdp_count, col_count), ('fs...  435 us
    reduce_scatter x1, waiting for transfers between devices, body(): lax.psum_scatter(spread_weight(grad_gate_attn_full, fsdp_count, col_count...  361 us
    reduce_scatter x1, waiting for transfers between devices, body(): lax.psum_scatter(spread_weight(grad_query_full, fsdp_count, col_count), (...  361 us
    reduce_scatter x1, waiting for transfers between devices, body(): lax.psum_scatter(spread_weight(grad_out_full, fsdp_count, col_count), ('f...  360 us
    reshape x14, local copies, waits for them, and re-layouts, assemble(): block_grid = gathered.reshape(fsdp_count, col_count, block_rows, block_cols)  285 us
    all_gather x2, waiting for transfers between devices, collect_ffn(): lax.all_gather(shards[2][None], ('fsdp', 'col'), axis=0, tiled=True)  253 us
  transfers between devices with their start and end apart: 28, of which 19 were waited for; matrix products, arithmetic and copies ran while one was open for 20% of the time, Pallas kernels for 0%

commit v1 on v0

v1 whole, which is shorter than its diff:
```python
import functools
import math

import jax
import jax.numpy as jnp
from jax import lax
from jax.experimental import pallas as pl
from jax.experimental.pallas import tpu as pltpu
from jax.sharding import Mesh
from jax.sharding import PartitionSpec as P

f32 = jnp.float32
bf16 = jnp.bfloat16
eps_norm = 1e-06
theta_base = 1000000.0
masked_score = -1e30
plane = ("x", "c", "y")
swap = [(0, 1), (1, 0)]
cross = [(0, 3), (3, 0), (1, 2), (2, 1)]


def dot(a, b, ca, cb, out=f32):
    return lax.dot_general(a, b, (((ca,), (cb,)), ((), ())), preferred_element_type=f32).astype(out)


def send_c(v):
    return lax.ppermute(v, "c", swap)


def send_x(v):
    return lax.ppermute(v, "x", swap)


def send_y(v):
    return lax.ppermute(v, "y", swap)


def send_xy(v):
    return lax.ppermute(v, ("x", "y"), cross)


def gather_plane(v):
    own = jnp.concatenate([v, send_y(v), send_x(v), send_xy(v)], axis=0)
    return own, send_c(own)


def reduce_plane(own, other):
    total = own + send_c(other).astype(f32)
    rows = own.shape[0] // 4
    part = [total[i * rows : (i + 1) * rows] for i in range(4)]
    low = [p.astype(bf16) for p in part]
    got = (send_y(low[1]), send_x(low[2]), send_xy(low[3]))
    return part[0] + got[0].astype(f32) + got[1].astype(f32) + got[2].astype(f32)


def doubling(v, axis, count, join):
    step = 1
    while step < count:
        v = join(v, lax.ppermute(v, axis, [(i, i ^ step) for i in range(count)]), step)
        step *= 2
    return v


def gather_rows(v, axis):
    count = lax.axis_size(axis)
    index = lax.axis_index(axis)

    def join(mine, theirs, step):
        low = (index & step) == 0
        return jnp.where(
            low,
            jnp.concatenate([mine, theirs], axis=0),
            jnp.concatenate([theirs, mine], axis=0),
        )

    return doubling(v, axis, count, join)


def sum_all(v, axis):
    return doubling(v, axis, lax.axis_size(axis), lambda a, b, step: a + b)


def rms_scale(values):
    return lax.rsqrt(jnp.mean(values * values, axis=-1, keepdims=True) + eps_norm)


def norm_back(grad, values, scale, gain):
    weighted = grad * gain
    inner = jnp.mean(weighted * values, axis=-1, keepdims=True)
    return scale * (weighted - values * (scale * scale) * inner), grad * values * scale


def angle_tables(positions, head_size):
    freq_index = jnp.arange(head_size // 2, dtype=f32)
    inverse = jnp.exp(freq_index * (-2.0 * math.log(theta_base) / head_size))
    angles = positions.astype(f32)[..., None] * inverse
    cosine, sine = jnp.cos(angles), jnp.sin(angles)
    return jnp.concatenate([cosine, cosine], -1), jnp.concatenate([-sine, sine], -1)


def softmax_rows(query, key, allowed, scale):
    scores = lax.dot_general(query, key, (((1,), (1,)), ((), ())), preferred_element_type=f32) * scale
    scores = jnp.where(allowed, scores, masked_score)
    shifted = jnp.exp(scores - jnp.max(scores, axis=-1, keepdims=True))
    return shifted / jnp.sum(shifted, axis=-1, keepdims=True)


def turn(values, cosine, sine):
    half = values.shape[-1] // 2
    return values * cosine + pltpu.roll(values, half, 1) * sine


def turn_back(grad, cosine, sine):
    half = grad.shape[-1] // 2
    return grad * cosine - pltpu.roll(grad, half, 1) * sine


def sigmoid(v):
    return 1.0 / (1.0 + jnp.exp(-v))


def load_rows(ref, low, high):
    part = ref[0, :, 0, :, low:high]
    return part.reshape(part.shape[0] * part.shape[1], high - low)


def store_rows(ref, low, high, value):
    _, halves, _, rows, _ = ref.shape
    ref[0, :, 0, :, low:high] = value.reshape(halves, rows, high - low)


def forward_kernel(size, group, proj, cos, sin, mask, gains, gated):
    scale = size ** (-0.5)
    cosine, sine = load_rows(cos, 0, size), load_rows(sin, 0, size)
    allowed = mask[0, 0] > 0.0
    wide = group * size
    key_raw = load_rows(proj, wide, wide + size)
    key = turn(key_raw * rms_scale(key_raw) * gains[1:2, :], cosine, sine).astype(bf16)
    value = load_rows(proj, wide + size, wide + 2 * size).astype(bf16)
    for h in range(group):
        low, high = h * size, (h + 1) * size
        query_raw = load_rows(proj, low, high)
        query = turn(query_raw * rms_scale(query_raw) * gains[0:1, :], cosine, sine).astype(bf16)
        prob = softmax_rows(query, key, allowed, scale).astype(bf16)
        mixed = jnp.dot(prob, value, preferred_element_type=f32)
        gate = sigmoid(load_rows(proj, wide + 2 * size + low, wide + 2 * size + high))
        store_rows(gated, low, high, (mixed * gate).astype(bf16))


def backward_kernel(size, group, proj, grad, cos, sin, mask, gains, out, gain_out):
    scale = size ** (-0.5)
    cosine, sine = load_rows(cos, 0, size), load_rows(sin, 0, size)
    allowed = mask[0, 0] > 0.0
    wide = group * size
    gain_q, gain_k = gains[0:1, :], gains[1:2, :]
    key_raw = load_rows(proj, wide, wide + size)
    key_scale = rms_scale(key_raw)
    key = turn(key_raw * key_scale * gain_k, cosine, sine).astype(bf16)
    value = load_rows(proj, wide + size, wide + 2 * size).astype(bf16)
    grad_key = jnp.zeros(key_raw.shape, f32)
    grad_value = jnp.zeros(key_raw.shape, f32)
    sum_q = jnp.zeros((1, size), f32)
    for h in range(group):
        low, high = h * size, (h + 1) * size
        query_raw = load_rows(proj, low, high)
        query_scale = rms_scale(query_raw)
        query = turn(query_raw * query_scale * gain_q, cosine, sine).astype(bf16)
        prob = softmax_rows(query, key, allowed, scale)
        prob_low = prob.astype(bf16)
        mixed = jnp.dot(prob_low, value, preferred_element_type=f32)
        gate = sigmoid(load_rows(proj, wide + 2 * size + low, wide + 2 * size + high))
        incoming = load_rows(grad, low, high)
        grad_mixed = (incoming * gate).astype(bf16)
        grad_gate = (incoming * mixed * gate * (1.0 - gate)).astype(bf16)
        store_rows(out, wide + 2 * size + low, wide + 2 * size + high, grad_gate)
        grad_prob = lax.dot_general(
            grad_mixed, value, (((1,), (1,)), ((), ())), preferred_element_type=f32
        )
        centre = jnp.sum(prob * grad_prob, axis=-1, keepdims=True)
        grad_score = (prob * (grad_prob - centre)).astype(bf16)
        grad_query = jnp.dot(grad_score, key, preferred_element_type=f32) * scale
        grad_key += lax.dot_general(
            grad_score, query, (((0,), (0,)), ((), ())), preferred_element_type=f32
        )
        grad_value += lax.dot_general(
            prob_low, grad_mixed, (((0,), (0,)), ((), ())), preferred_element_type=f32
        )
        raw, addend = norm_back(turn_back(grad_query, cosine, sine), query_raw, query_scale, gain_q)
        sum_q += jnp.sum(addend, axis=0, keepdims=True)
        store_rows(out, low, high, raw.astype(bf16))
    raw, addend = norm_back(turn_back(grad_key * scale, cosine, sine), key_raw, key_scale, gain_k)
    store_rows(out, wide, wide + size, raw.astype(bf16))
    store_rows(out, wide + size, wide + 2 * size, grad_value.astype(bf16))
    gain_out[0, 0, 0:1, :] = sum_q
    gain_out[0, 0, 1:2, :] = jnp.sum(addend, axis=0, keepdims=True)


def rows_spec(micro, rows, width):
    return pl.BlockSpec((1, 2, 1, rows, width), lambda i, m: (i, 0, m, 0, 0))


def attention_forward(proj, tables, gains, group, micro):
    cos, sin, mask = tables
    rows, size = cos.shape[3], cos.shape[4]
    view = proj.reshape(2, 2, micro, rows, proj.shape[1])
    spec = functools.partial(rows_spec, micro, rows)
    out = pl.pallas_call(
        functools.partial(forward_kernel, size, group),
        grid=(2, micro),
        in_specs=[
            spec(proj.shape[1]),
            spec(size),
            spec(size),
            pl.BlockSpec((1, 1, 2 * rows, 2 * rows), lambda i, m: (i, m, 0, 0)),
            pl.BlockSpec((2, size), lambda i, m: (0, 0)),
        ],
        out_specs=spec(group * size),
        out_shape=jax.ShapeDtypeStruct((2, 2, micro, rows, group * size), bf16),
        name="attn_fwd",
    )(view, cos, sin, mask, gains)
    return out.reshape(proj.shape[0], group * size)


def attention_backward(proj, grad, tables, gains, group, micro):
    cos, sin, mask = tables
    rows, size = cos.shape[3], cos.shape[4]
    spec = functools.partial(rows_spec, micro, rows)
    out, sums = pl.pallas_call(
        functools.partial(backward_kernel, size, group),
        grid=(2, micro),
        in_specs=[
            spec(proj.shape[1]),
            spec(group * size),
            spec(size),
            spec(size),
            pl.BlockSpec((1, 1, 2 * rows, 2 * rows), lambda i, m: (i, m, 0, 0)),
            pl.BlockSpec((2, size), lambda i, m: (0, 0)),
        ],
        out_specs=[
            spec(proj.shape[1]),
            pl.BlockSpec((1, 1, 2, size), lambda i, m: (i, m, 0, 0)),
        ],
        out_shape=[
            jax.ShapeDtypeStruct((2, 2, micro, rows, proj.shape[1]), bf16),
            jax.ShapeDtypeStruct((2, micro, 2, size), f32),
        ],
        name="attn_bwd",
    )(
        proj.reshape(2, 2, micro, rows, proj.shape[1]),
        grad.reshape(2, 2, micro, rows, grad.shape[1]),
        cos,
        sin,
        mask,
        gains,
    )
    return out.reshape(proj.shape), jnp.sum(sums, axis=(0, 1))


def make_tables(lengths, side, rows, size):
    inner = jnp.arange(rows, dtype=jnp.int32)
    position = jnp.concatenate([side * rows + inner, (1 - side) * rows + inner])
    ends = jnp.cumsum(lengths, axis=-1, dtype=jnp.int32)
    passed = position[None, None, :, None] >= ends[:, :, None, :]
    doc = jnp.sum(passed.astype(jnp.int32), axis=-1, dtype=jnp.int32)
    starts = jnp.sum(jnp.where(passed, lengths[:, :, None, :], 0), axis=-1, dtype=jnp.int32)
    cos, sin = angle_tables(position - starts, size)
    mask = (doc[:, :, :, None] == doc[:, :, None, :]) & (position[None, :] <= position[:, None])

    def halves(v):
        return v.reshape(2, v.shape[1], 2, rows, size).transpose(0, 2, 1, 3, 4)

    return halves(cos), halves(sin), mask.astype(f32)


def pack_columns(mats):
    parts = [m.reshape(m.shape[0], 4, m.shape[1] // 4) for m in mats]
    return jnp.concatenate(parts, axis=2).transpose(1, 0, 2)


def share_columns(mats):
    packed = lax.all_to_all(pack_columns(mats), ("x", "c"), split_axis=0, concat_axis=0, tiled=True)
    packed = packed.reshape(packed.shape[0] * packed.shape[1], packed.shape[2])
    return lax.all_gather(packed, "g", axis=0, tiled=True)


def return_columns(grad, widths):
    mine = lax.psum_scatter(grad, "g", scatter_dimension=0, tiled=True)
    blocks = mine.reshape(4, mine.shape[0] // 4, mine.shape[1])
    got = lax.all_to_all(blocks, ("x", "c"), split_axis=0, concat_axis=0, tiled=True)
    outs, low = [], 0
    for width in widths:
        part = got[:, :, low : low + width].transpose(1, 0, 2)
        outs.append(part.reshape(part.shape[0], 4 * width).astype(f32))
        low += width
    return outs


def row_route(group_count, col_count):
    per = group_count // col_count
    pairs = []
    for f in range(4 * group_count):
        for y in range(col_count):
            block, inner = f // per, f % per
            target = inner * col_count + y
            y_to, rest = block // 4, block % 4
            pairs.append((f * col_count + y, (target * 4 + rest) * col_count + y_to))
    return pairs


every = ("g", "x", "c", "y")


def share_rows(mat, route, col_count):
    moved = lax.ppermute(mat, every, route)
    full = lax.all_gather(moved[None], "g", axis=0, tiled=True)
    count, rows, cols = full.shape
    full = full.reshape(count // col_count, col_count, rows, cols).transpose(0, 2, 1, 3)
    return full.reshape(count // col_count * rows, col_count * cols)


def return_rows(grad, route, group_count, col_count):
    per = group_count // col_count
    rows, cols = grad.shape[0] // per, grad.shape[1] // col_count
    blocks = grad.reshape(per, rows, col_count, cols).transpose(0, 2, 1, 3)
    blocks = blocks.reshape(group_count * rows, cols)
    mine = lax.psum_scatter(blocks, "g", scatter_dimension=0, tiled=True)
    return lax.ppermute(mine, every, [(b, a) for a, b in route]).astype(f32)


def body(
    block_input,
    doc_lengths,
    norm_attn,
    w_query,
    w_key,
    w_value,
    w_gate_attn,
    w_out,
    gain_query,
    gain_key,
    norm_ffn,
    w_gate,
    w_up,
    w_down,
    grad_output,
):
    group_count, col_count = lax.axis_size("g"), lax.axis_size("y")
    fsdp_count = 4 * group_count
    side = lax.axis_index("y")
    owner = lax.axis_index("g") * 4 + lax.axis_index("x") * 2 + lax.axis_index("c")
    micro, _, rows, width = block_input.shape
    size = gain_query.shape[0] * fsdp_count
    group = w_query.shape[1] // w_key.shape[1]
    route = row_route(group_count, col_count)

    tokens_low = block_input.reshape(micro * rows, width)
    cotangent = grad_output.reshape(micro * rows, width)

    token_pair = gather_plane(tokens_low)
    packed = jnp.concatenate([norm_attn, norm_ffn, gain_query, gain_key])[None]
    every_gain = gather_rows(gather_rows(gather_rows(packed, "c"), "x"), "g").astype(f32)
    piece, small = norm_attn.shape[0], gain_query.shape[0]
    gain_one = every_gain[:, :piece].reshape(1, width)
    gain_two = every_gain[:, piece : 2 * piece].reshape(1, width)
    gain_q = every_gain[:, 2 * piece : 2 * piece + small].reshape(1, size)
    gain_k = every_gain[:, 2 * piece + small :].reshape(1, size)
    head_gains = jnp.concatenate([gain_q, gain_k], axis=0)
    lengths = doc_lengths.reshape(1, micro, doc_lengths.shape[2])
    lengths = jnp.concatenate([lengths, send_x(lengths)], axis=0)
    tables = [make_tables(v, side, rows, size) for v in (lengths, send_c(lengths))]

    qkvg = share_columns((w_query, w_key, w_value, w_gate_attn))
    out_rows = share_rows(w_out, route, col_count)
    gate_up = share_columns((w_gate, w_up))
    down_rows = share_rows(w_down, route, col_count)
    cot_pair = gather_plane(cotangent)

    def first_norm(v):
        v = v.astype(f32)
        return (v * rms_scale(v) * gain_one).astype(bf16)

    hidden = [first_norm(v) for v in token_pair]
    proj = [dot(h, qkvg, 1, 0) for h in hidden]
    gated = [attention_forward(p, t, head_gains, group, micro) for p, t in zip(proj, tables)]
    mixed = reduce_plane(dot(gated[0], out_rows, 1, 0), dot(gated[1], out_rows, 1, 0, bf16))
    tokens = tokens_low.astype(f32)
    residual = tokens + mixed
    scale_two = rms_scale(residual)
    hidden_two = gather_plane((residual * scale_two * gain_two).astype(bf16))
    units = gate_up.shape[1] // 2

    inner, grad_units = [], []
    for h, g in zip(hidden_two, cot_pair):
        pre = dot(h, gate_up, 1, 0)
        gate_pre, up_pre = pre[:, :units], pre[:, units:]
        grad_inner = dot(g, down_rows, 1, 1)
        sig = jax.nn.sigmoid(gate_pre)
        act = gate_pre * sig
        inner.append((act * up_pre).astype(bf16))
        grad_gate = grad_inner * up_pre * (sig * (1.0 + gate_pre * (1.0 - sig)))
        grad_units.append(
            jnp.concatenate([grad_gate.astype(bf16), (grad_inner * act).astype(bf16)], axis=1)
        )
    grad_hidden_two = reduce_plane(
        dot(grad_units[0], gate_up, 1, 1), dot(grad_units[1], gate_up, 1, 1, bf16)
    )
    final = reduce_plane(dot(inner[0], down_rows, 1, 0), dot(inner[1], down_rows, 1, 0, bf16))
    block_output = (residual + final).astype(bf16).reshape(block_input.shape)

    def weight_grad(left, right):
        return (dot(left[0], right[0], 0, 0) + dot(left[1], right[1], 0, 0)).astype(bf16)

    grad_down = return_rows(weight_grad(inner, cot_pair), route, group_count, col_count)
    grad_gate, grad_up = return_columns(
        weight_grad(hidden_two, grad_units), (units, units)
    )

    back, addend = norm_back(grad_hidden_two, residual, scale_two, gain_two)
    sum_two = jnp.sum(addend, axis=0)
    grad_resid = cotangent.astype(f32) + back
    low_pair = gather_plane(grad_resid.astype(bf16))
    grad_gated = [dot(d, out_rows, 1, 1) for d in low_pair]
    backs = [
        attention_backward(p, d, t, head_gains, group, micro)
        for p, d, t in zip(proj, grad_gated, tables)
    ]
    grad_proj = [b[0] for b in backs]
    grad_hidden = reduce_plane(dot(grad_proj[0], qkvg, 1, 1), dot(grad_proj[1], qkvg, 1, 1, bf16))
    grad_out = return_rows(weight_grad(gated, low_pair), route, group_count, col_count)
    query_width, key_width = group * size, size
    grad_query, grad_key, grad_value, grad_gate_attn = return_columns(
        weight_grad(hidden, grad_proj), (query_width, key_width, key_width, query_width)
    )
    back, addend = norm_back(grad_hidden, tokens, rms_scale(tokens), gain_one)
    grad_input = (grad_resid + back).reshape(block_input.shape)

    head_sums = backs[0][1] + backs[1][1]
    sums = jnp.concatenate(
        [
            jnp.sum(addend, axis=0).reshape(fsdp_count, piece),
            sum_two.reshape(fsdp_count, piece),
            head_sums[0].reshape(fsdp_count, small),
            head_sums[1].reshape(fsdp_count, small),
        ],
        axis=1,
    )
    for axis in ("c", "y", "x", "g"):
        sums = sum_all(sums, axis)
    mine = lax.dynamic_index_in_dim(sums, owner, 0, keepdims=False)
    return (
        block_output,
        grad_input,
        mine[:piece],
        grad_query,
        grad_key,
        grad_value,
        grad_gate_attn,
        grad_out,
        mine[2 * piece : 2 * piece + small],
        mine[2 * piece + small :],
        mine[piece : 2 * piece],
        grad_gate,
        grad_up,
        grad_down,
    )


def solution(mesh):
    fsdp_count, col_count = mesh.shape["fsdp"], mesh.shape["col"]
    grid = Mesh(mesh.devices.reshape(fsdp_count // 4, 2, 2, col_count), every)
    rows = ("g", "x", "c")
    token, vector, matrix = P(None, rows, "y", None), P(rows), P(rows, "y")
    in_specs = (
        (token, P(None, rows, None), vector)
        + (matrix,) * 5
        + (vector,) * 3
        + (matrix,) * 3
        + (token,)
    )
    out_specs = (token, token, vector) + (matrix,) * 5 + (vector,) * 3 + (matrix,) * 3
    return jax.shard_map(body, mesh=grid, in_specs=in_specs, out_specs=out_specs, check_vma=False)
```

time: 4570 us -> 774 us (0.17)
  waiting for transfers between devices: 3310 us -> 388 us
  local copies, waits for them, and re-layouts: 701 us -> 45.1 us
  blocking collectives: 215 us -> 29.2 us
  matrix products: 275 us -> 105 us
  starting transfers between devices: 7.06 us -> 123 us
    reduce_scatter x8 -> x4, waiting for transfers between devices: 2410 us -> 118 us  [the longest x2 90.2 us: return_columns(): mine = lax.psum_scatter(grad, 'g', scatter_dimension=0, tiled=True)]
    all_gather x16 -> x4, waiting for transfers between devices: 886 us -> 59.4 us  [the longest x2 59.4 us: share_columns(): return lax.all_gather(packed, 'g', axis=0, tiled=True)]
    reshape x27 -> x7, local copies, waits for them, and re-layouts: 435 us -> 15.8 us  [the longest x2 7.46 us: share_rows(): full.reshape(count // col_count, col_count, rows, cols)]
    ppermute x4 -> x47, waiting for transfers between devices: 3.88 us -> 198 us  [the longest x9 96 us: send_x(): return lax.ppermute(v, 'x', swap)]
    dot_general x80 -> x24, matrix products: 275 us -> 105 us  [dot(): lax.dot_general(a, b, (((ca,), (cb,)), ((), ())), preferred_element_type=...]
    all_gather x2 -> x0, blocking collectives: 136 us -> none  [the longest x1 70.1 us: collect_attention(): lax.all_gather(shards[0][None], ('fsdp', 'col'), axis=0, tiled=True)]
    transpose x6 -> x2, local copies, waits for them, and re-layouts: 130 us -> 5.75 us  [return_rows(): blocks = grad.reshape(per, rows, col_count, cols).transpose(0, 2, 1, 3)]
    ppermute x4 -> x47, starting transfers between devices: 6.12 us -> 112 us  [the longest x9 43.2 us: doubling(): lax.ppermute(v, axis, [(i, i ^ step) for i in range(count)])]
  transfers between devices with their start and end apart: 28 -> 58, of which waited for: 19 -> 30; matrix products, arithmetic and copies ran while one was open for 20% -> 22% of each run, Pallas kernels for 0% -> 4%
where the time goes in v1:
time: 774 us; the launch traced here: 766 us
  waiting for transfers between devices  388 us (50%)
  starting transfers between devices  123 us (16%)
  matrix products  105 us (14%)
  local copies, waits for them, and re-layouts  45.1 us (6%)
  other arithmetic  30.6 us (4%)
  Pallas kernels  29.5 us (4%)
  blocking collectives  29.2 us (4%)
  between operations  15.5 us (2%)
    dot_general x24, matrix products, dot(): lax.dot_general(a, b, (((ca,), (cb,)), ((), ())), preferred_element_type=...  105 us
    ppermute x9, waiting for transfers between devices, send_x(): return lax.ppermute(v, 'x', swap)  96 us
    reduce_scatter x2, waiting for transfers between devices, return_columns(): mine = lax.psum_scatter(grad, 'g', scatter_dimension=0, tiled=True)  90.2 us
    ppermute x8, waiting for transfers between devices, send_xy(): return lax.ppermute(v, ('x', 'y'), cross)  76.7 us
    all_gather x2, waiting for transfers between devices, share_columns(): return lax.all_gather(packed, 'g', axis=0, tiled=True)  59.4 us
    ppermute x9, starting transfers between devices, doubling(): lax.ppermute(v, axis, [(i, i ^ step) for i in range(count)])  43.2 us
    ppermute x8, starting transfers between devices, send_xy(): return lax.ppermute(v, ('x', 'y'), cross)  42.9 us
    all_to_all x1, blocking collectives, share_columns(): lax.all_to_all(pack_columns(mats), ('x', 'c'), split_axis=0, concat_axis=...  29.2 us
  transfers between devices with their start and end apart: 58, of which 30 were waited for; matrix products, arithmetic and copies ran while one was open for 22% of the time, Pallas kernels for 4%

profile of v1, /device:TPU:0, one launch (start us, length us, event | category | flops | bytes accessed | tf_op | source)
XLA Modules:
  0.0 765.9 jit_solution(12796806292681625462)
XLA Ops:
  14.1 29.2 %all_to_all.20 = bf16[4,128,768]{1,2,0:T(8,128)(2,1)S(1)} all-to-all(bf16[4,128,768]{1,2,0:T(8,128)(2,1)S(1)} %maximum_bitcast_fusion.1), channel_id=1, replica_groups=mesh['g'=4,'x'=2,'c'=2,'y'=2] {'x','c'}, dimensions={0} | all-to-all | bytes 1572864 | tf_op jit(solution)/shard_map/all_to_all | solution.py:281
  47.2 26.1 %collective-permute-start.2 = (bf16[128,2048]{1,0:T(8,128)(2,1)S(1)}, bf16[128,2048]{1,0:T(8,128)(2,1)S(1)}, u32[]{:S(2)}, u32[]{:S(2)}) collective-permute-start(bf16[128,2048]{1,0:T(8,128)(2,1)S(1)} %bitcast.142), channel_id=1, source_target_pairs={{0,5},{5,0},{1,4},{4,1},{2,7},{7,2},{3,6},{6,3},{8,13},{13,8},{9,1... | collective-permute-start | bytes 1572872 | tf_op jit(solution)/shard_map/ppermute | solution.py:39
  88.1 14.5 %collective-permute-done.7 = s32[1,2,4]{2,1,0:T(2,128)S(1)} collective-permute-done((s32[1,2,4]{2,1,0:T(2,128)S(1)}, s32[1,2,4]{2,1,0:T(2,128)S(1)}, u32[]{:S(2)}, u32[]{:S(2)}) %collective-permute-start.7) | collective-permute-done | bytes 64 | tf_op jit(solution)/shard_map/ppermute | solution.py:31
  167.1 12.2 %collective-permute-done.14 = bf16[128,2048]{1,0:T(8,128)(2,1)S(1)} collective-permute-done((bf16[128,2048]{1,0:T(8,128)(2,1)S(1)}, bf16[128,2048]{1,0:T(8,128)(2,1)S(1)}, u32[]{:S(2)}, u32[]{:S(2)}) %collective-permute-start.14) | collective-permute-done | bytes 524320 | tf_op jit(solution)/shard_map/ppermute | solution.py:39
  179.4 10.7 %collective-permute-done.13 = bf16[128,2048]{1,0:T(8,128)(2,1)S(1)} collective-permute-done((bf16[128,2048]{1,0:T(8,128)(2,1)S(1)}, bf16[128,2048]{1,0:T(8,128)(2,1)S(1)}, u32[]{:S(2)}, u32[]{:S(2)}) %collective-permute-start.13) | collective-permute-done | bytes 524320 | tf_op jit(solution)/shard_map/ppermute | solution.py:31
  194.4 12.2 %collective-permute-done.17 = bf16[128,2048]{1,0:T(8,128)(2,1)S(1)} collective-permute-done((bf16[128,2048]{1,0:T(8,128)(2,1)S(1)}, bf16[128,2048]{1,0:T(8,128)(2,1)S(1)}, u32[]{:S(2)}, u32[]{:S(2)}) %collective-permute-start.17) | collective-permute-done | bytes 524320 | tf_op jit(solution)/shard_map/ppermute | solution.py:39
  206.6 10.3 %collective-permute-done.16 = bf16[128,2048]{1,0:T(8,128)(2,1)S(1)} collective-permute-done((bf16[128,2048]{1,0:T(8,128)(2,1)S(1)}, bf16[128,2048]{1,0:T(8,128)(2,1)S(1)}, u32[]{:S(2)}, u32[]{:S(2)}) %collective-permute-start.16) | collective-permute-done | bytes 524320 | tf_op jit(solution)/shard_map/ppermute | solution.py:31
  222.3 12.2 %collective-permute-done.26 = bf16[128,2048]{1,0:T(8,128)(2,1)S(1)} collective-permute-done((bf16[128,2048]{1,0:T(8,128)(2,1)S(1)}, bf16[128,2048]{1,0:T(8,128)(2,1)S(1)}, u32[]{:S(2)}, u32[]{:S(2)}) %collective-permute-start.26) | collective-permute-done | bytes 524320 | tf_op jit(solution)/shard_map/ppermute | solution.py:39
  234.6 10.6 %collective-permute-done.25 = bf16[128,2048]{1,0:T(8,128)(2,1)S(1)} collective-permute-done((bf16[128,2048]{1,0:T(8,128)(2,1)S(1)}, bf16[128,2048]{1,0:T(8,128)(2,1)S(1)}, u32[]{:S(2)}, u32[]{:S(2)}) %collective-permute-start.25) | collective-permute-done | bytes 524320 | tf_op jit(solution)/shard_map/ppermute | solution.py:31
  254.8 59.0 %all-gather.9.cloned.1.call-done = bf16[2048,1536]{1,0:T(8,128)(2,1)} async-done(((bf16[512,1536]{1,0:T(8,128)(2,1)}), bf16[2048,1536]{1,0:T(8,128)(2,1)}) %all-gather.9.cloned.1.call-update) | async-done | bytes 6291472 | tf_op jit(solution)/shard_map/all_gather | solution.py:283
  384.1 9.8 %collective-permute-done.30 = bf16[128,2048]{1,0:T(8,128)(2,1)S(1)} collective-permute-done((bf16[128,2048]{1,0:T(8,128)(2,1)S(1)}, bf16[128,2048]{1,0:T(8,128)(2,1)S(1)}, u32[]{:S(2)}, u32[]{:S(2)}) %collective-permute-start.30) | collective-permute-done | bytes 524320 | tf_op jit(solution)/shard_map/ppermute | solution.py:31
  394.6 10.6 %collective-permute-done.23 = bf16[128,2048]{1,0:T(8,128)(2,1)S(1)} collective-permute-done((bf16[128,2048]{1,0:T(8,128)(2,1)S(1)}, bf16[128,2048]{1,0:T(8,128)(2,1)S(1)}, u32[]{:S(2)}, u32[]{:S(2)}) %collective-permute-start.23) | collective-permute-done | bytes 524320 | tf_op jit(solution)/shard_map/ppermute | solution.py:39
  405.2 10.3 %collective-permute-done.22 = bf16[128,2048]{1,0:T(8,128)(2,1)S(1)} collective-permute-done((bf16[128,2048]{1,0:T(8,128)(2,1)S(1)}, bf16[128,2048]{1,0:T(8,128)(2,1)S(1)}, u32[]{:S(2)}, u32[]{:S(2)}) %collective-permute-start.22) | collective-permute-done | bytes 524320 | tf_op jit(solution)/shard_map/ppermute | solution.py:31
  420.9 12.2 %collective-permute-done.34 = bf16[128,2048]{1,0:T(8,128)(2,1)S(1)} collective-permute-done((bf16[128,2048]{1,0:T(8,128)(2,1)S(1)}, bf16[128,2048]{1,0:T(8,128)(2,1)S(1)}, u32[]{:S(2)}, u32[]{:S(2)}) %collective-permute-start.34) | collective-permute-done | bytes 524320 | tf_op jit(solution)/shard_map/ppermute | solution.py:39
  433.1 10.3 %collective-permute-done.33 = bf16[128,2048]{1,0:T(8,128)(2,1)S(1)} collective-permute-done((bf16[128,2048]{1,0:T(8,128)(2,1)S(1)}, bf16[128,2048]{1,0:T(8,128)(2,1)S(1)}, u32[]{:S(2)}, u32[]{:S(2)}) %collective-permute-start.33) | collective-permute-done | bytes 524320 | tf_op jit(solution)/shard_map/ppermute | solution.py:31
  449.4 8.8 %attn_bwd.2 = (bf16[2,2,2,64,768]{4,3,2,1,0:T(8,128)(2,1)}, f32[2,2,2,128]{3,2,1,0:T(2,128)}) custom-call(f32[2,2,2,64,768]{4,3,2,1,0:T(8,128)} %bitcast.161, f32[2,2,2,64,256]{4,3,2,1,0:T(8,128)} %fusion.28.grad, f32[2,2,2,64,128]{4,3,2,1,0:T(8,128)} %maximum_bitcast_fusion.2.cos, f32[2,2,2,64,128]{4,3,2,1,0:T(8,128)} %maximum_bitcast_fusion.3.sin, ...), custom_call_target="tpu_custom_call" | custom-call | tf_op jit(solution)/shard_map/attn_bwd/pallas_call | solution.py:228
  486.0 10.2 %fusion.30 = f32[2048,1536]{1,0:T(8,128)} fusion(bf16[512,2048]{1,0:T(8,128)(2,1)} %collective-permute-done.19, bf16[512,768]{1,0:T(8,128)(2,1)} %copy-done.54, bf16[512,768]{1,0:T(8,128)(2,1)} %copy-done.53), kind=kOutput, calls=%fused_computation.77 | convolution fusion | flops 3224371200 | bytes 16252928 | tf_op jit(solution)/shard_map/dot_general | solution.py:23
  524.7 11.5 %collective-permute-done.39 = bf16[128,2048]{1,0:T(8,128)(2,1)S(1)} collective-permute-done((bf16[128,2048]{1,0:T(8,128)(2,1)}, bf16[128,2048]{1,0:T(8,128)(2,1)S(1)}, u32[]{:S(2)}, u32[]{:S(2)}) %collective-permute-start.39) | collective-permute-done | bytes 524320 | tf_op jit(solution)/shard_map/ppermute | solution.py:39
  536.3 19.5 %collective-permute-done.38 = bf16[128,2048]{1,0:T(8,128)(2,1)S(1)} collective-permute-done((bf16[128,2048]{1,0:T(8,128)(2,1)}, bf16[128,2048]{1,0:T(8,128)(2,1)S(1)}, u32[]{:S(2)}, u32[]{:S(2)}) %collective-permute-start.38) | collective-permute-done | bytes 524320 | tf_op jit(solution)/shard_map/ppermute | solution.py:31
  558.4 16.0 %reduce-scatter.5.cloned.1.call-done = bf16[512,768]{1,0:T(8,128)(2,1)} async-done(((bf16[2048,768]{1,0:T(8,128)(2,1)}), bf16[512,768]{1,0:T(8,128)(2,1)}) %reduce-scatter.5.cloned.1.call-update) | async-done | bytes 786448 | tf_op jit(solution)/shard_map/reduce_scatter | solution.py:287
  578.5 27.3 %reduce-scatter.7.cloned.1.call-done = bf16[128,1024]{1,0:T(8,128)(2,1)} async-done(((bf16[512,1024]{1,0:T(8,128)(2,1)}), bf16[128,1024]{1,0:T(8,128)(2,1)}) %reduce-scatter.7.cloned.1.call-update) | async-done | bytes 262160 | tf_op jit(solution)/shard_map/reduce_scatter | solution.py:326
  615.8 35.3 %collective-permute-start.43 = (f32[16,272]{1,0:T(8,128)S(1)}, f32[16,272]{1,0:T(8,128)S(1)}, u32[]{:S(2)}, u32[]{:S(2)}) collective-permute-start(f32[16,272]{1,0:T(8,128)S(1)} %add.210), channel_id=1, source_target_pairs={{0,8},{8,0},{16,24},{24,16},{1,9},{9,1},{17,25},{25,17},{2,10},{10... | collective-permute-start | bytes 52232 | tf_op jit(solution)/shard_map/ppermute | solution.py:59
  657.9 74.2 %reduce-scatter.9.cloned.1.call-done = bf16[512,1536]{1,0:T(8,128)(2,1)} async-done(((bf16[2048,1536]{1,0:T(8,128)(2,1)}), bf16[512,1536]{1,0:T(8,128)(2,1)}) %reduce-scatter.9.cloned.1.call-update) | async-done | bytes 1572880 | tf_op jit(solution)/shard_map/reduce_scatter | solution.py:287
  742.9 12.8 %all-to-all-done.3 = bf16[4,128,1536]{2,1,0:T(8,128)(2,1)S(1)} async-done(((bf16[4,128,1536]{2,1,0:T(8,128)(2,1)}), bf16[4,128,1536]{2,1,0:T(8,128)(2,1)S(1)}, u32[]{:S(2)}, u32[]{:S(2)}) %all-to-all-start.3) | async-done | bytes 1572896 | tf_op jit(solution)/shard_map/all_to_all | solution.py:289
  (342 shorter events, 284.4 us)
Async XLA Ops:
  7.2 121.9 %all-gather.11.cloned.1.call-start = ((), (), s32[]{:S(2)}) async-start(), calls=%async_computation.14 | async-start | bytes 1310720 | tf_op jit(solution)/shard_map/all_gather | solution.py:315
  9.6 124.6 %all-gather.7.cloned.1.call-start = ((), (), s32[]{:S(2)}) async-start(), calls=%async_computation.8 | async-start | bytes 3932160 | tf_op jit(solution)/shard_map/all_gather | solution.py:283
  44.4 202.6 %all-gather.13.cloned.1.call-start = ((), (), s32[]{:S(2)}) async-start(), calls=%async_computation.15 | async-start | bytes 3932160 | tf_op jit(solution)/shard_map/all_gather | solution.py:315
  47.2 57.0 %collective-permute-start.2 = (bf16[128,2048]{1,0:T(8,128)(2,1)S(1)}, bf16[128,2048]{1,0:T(8,128)(2,1)S(1)}, u32[]{:S(2)}, u32[]{:S(2)}) collective-permute-start(bf16[128,2048]{1,0:T(8,128)(2,1)S(1)} %bitcast.142), channel_id=1, source_target_pairs={{0,5},{5,0},{1,4},{4,1},{2,7},{7,2},{3,6},{6,3},{8,13},{13,8},{9,1... | collective-permute-start | bytes 1572872 | tf_op jit(solution)/shard_map/ppermute | solution.py:39
  73.3 30.9 %collective-permute-start.1 = (bf16[128,2048]{1,0:T(8,128)(2,1)S(1)}, bf16[128,2048]{1,0:T(8,128)(2,1)}, u32[]{:S(2)}, u32[]{:S(2)}) collective-permute-start(bf16[128,2048]{1,0:T(8,128)(2,1)S(1)} %bitcast.143), channel_id=1, source_target_pairs={{0,4},{4,0},{1,5},{5,1},{2,6},{6,2},{3,7},{7,3},{8,12},{12,8},{9,1... | collective-permute-start | bytes 1572872 | tf_op jit(solution)/shard_map/ppermute | solution.py:31
  84.2 42.2 %all-to-all-start.1 = ((bf16[4,128,1536]{1,2,0:T(8,128)(2,1)}), bf16[4,128,1536]{1,2,0:T(8,128)(2,1)S(1)}, u32[]{:S(2)}, u32[]{:S(2)}) async-start(bf16[4,128,1536]{1,2,0:T(8,128)(2,1)} %maximum_bitcast_fusion), calls=%async_computation.1 | async-start | bytes 3145728 | tf_op jit(solution)/shard_map/all_to_all | solution.py:281
  87.8 226.0 %all-gather.9.cloned.1.call-start = ((), (), s32[]{:S(2)}) async-start(), calls=%async_computation.9 | async-start | bytes 7864320 | tf_op jit(solution)/shard_map/all_gather | solution.py:283
  128.0 394.8 %reduce-scatter.11.cloned.1.call-start = ((), (), s32[]{:S(2)}) async-start(), calls=%async_computation.13 | async-start | bytes 3932160 | tf_op jit(solution)/shard_map/reduce_scatter | solution.py:326
  218.7 36.1 %collective-permute-start.19 = (bf16[512,2048]{1,0:T(8,128)(2,1)}, bf16[512,2048]{1,0:T(8,128)(2,1)}, u32[]{:S(2)}, u32[]{:S(2)}) collective-permute-start(bf16[512,2048]{1,0:T(8,128)(2,1)} %pad_maximum_fusion.1), channel_id=1, source_target_pairs={{0,2},{2,0},{1,3},{3,1},{4,6},{6,4},{5,7},{7,5},{8,10},{10,8},{9,1... | collective-permute-start | bytes 6291464 | tf_op jit(solution)/shard_map/ppermute | solution.py:27
  246.8 73.7 %collective-permute-start.27 = (bf16[512,2048]{1,0:T(8,128)(2,1)}, bf16[512,2048]{1,0:T(8,128)(2,1)}, u32[]{:S(2)}, u32[]{:S(2)}) collective-permute-start(bf16[512,2048]{1,0:T(8,128)(2,1)} %pad_maximum_fusion.2), channel_id=1, source_target_pairs={{0,2},{2,0},{1,3},{3,1},{4,6},{6,4},{5,7},{7,5},{8,10},{10,8},{9,1... | collective-permute-start | bytes 6291464 | tf_op jit(solution)/shard_map/ppermute | solution.py:27
  329.4 29.9 %collective-permute-start.28 = (bf16[512,2048]{1,0:T(8,128)(2,1)}, bf16[512,2048]{1,0:T(8,128)(2,1)}, u32[]{:S(2)}, u32[]{:S(2)}) collective-permute-start(bf16[512,2048]{1,0:T(8,128)(2,1)} %convolution_convert_fusion.2), channel_id=1, source_target_pairs={{0,2},{2,0},{1,3},{3,1},{4,6},{6,4},{5,7},{7,5},{8,10},{10,8},{9,1... | collective-permute-start | bytes 6291464 | tf_op jit(solution)/shard_map/ppermute | solution.py:27
  332.6 37.8 %collective-permute-start.20 = (bf16[512,2048]{1,0:T(8,128)(2,1)}, bf16[512,2048]{1,0:T(8,128)(2,1)}, u32[]{:S(2)}, u32[]{:S(2)}) collective-permute-start(bf16[512,2048]{1,0:T(8,128)(2,1)} %convolution_convert_fusion.3), channel_id=1, source_target_pairs={{0,2},{2,0},{1,3},{3,1},{4,6},{6,4},{5,7},{7,5},{8,10},{10,8},{9,1... | collective-permute-start | bytes 6291464 | tf_op jit(solution)/shard_map/ppermute | solution.py:27
  359.2 215.2 %reduce-scatter.5.cloned.1.call-start = ((), (), s32[]{:S(2)}) async-start(), calls=%async_computation.10 | async-start | bytes 3932160 | tf_op jit(solution)/shard_map/reduce_scatter | solution.py:287
  374.0 31.2 %collective-permute-start.23 = (bf16[128,2048]{1,0:T(8,128)(2,1)S(1)}, bf16[128,2048]{1,0:T(8,128)(2,1)S(1)}, u32[]{:S(2)}, u32[]{:S(2)}) collective-permute-start(bf16[128,2048]{1,0:T(8,128)(2,1)S(1)} %get-tuple-element.117), channel_id=1, source_target_pairs={{0,5},{5,0},{1,4},{4,1},{2,7},{7,2},{3,6},{6,3},{8,13},{13,8},{9,1... | collective-permute-start | bytes 1572872 | tf_op jit(solution)/shard_map/ppermute | solution.py:39
  376.5 39.0 %collective-permute-start.22 = (bf16[128,2048]{1,0:T(8,128)(2,1)S(1)}, bf16[128,2048]{1,0:T(8,128)(2,1)S(1)}, u32[]{:S(2)}, u32[]{:S(2)}) collective-permute-start(bf16[128,2048]{1,0:T(8,128)(2,1)S(1)} %get-tuple-element.118), channel_id=1, source_target_pairs={{0,4},{4,0},{1,5},{5,1},{2,6},{6,2},{3,7},{7,3},{8,12},{12,8},{9,1... | collective-permute-start | bytes 1572872 | tf_op jit(solution)/shard_map/ppermute | solution.py:31
  382.6 32.8 %collective-permute-start.21 = (bf16[128,2048]{1,0:T(8,128)(2,1)S(1)}, bf16[128,2048]{1,0:T(8,128)(2,1)S(1)}, u32[]{:S(2)}, u32[]{:S(2)}) collective-permute-start(bf16[128,2048]{1,0:T(8,128)(2,1)S(1)} %get-tuple-element.116), channel_id=1, source_target_pairs={{0,1},{1,0},{2,3},{3,2},{4,5},{5,4},{6,7},{7,6},{8,9},{9,8},{10,11... | collective-permute-start | bytes 1572872 | tf_op jit(solution)/shard_map/ppermute | solution.py:35
  479.4 126.4 %reduce-scatter.7.cloned.1.call-start = ((), (), s32[]{:S(2)}) async-start(), calls=%async_computation.11 | async-start | bytes 1310720 | tf_op jit(solution)/shard_map/reduce_scatter | solution.py:326
  485.7 246.4 %reduce-scatter.9.cloned.1.call-start = ((), (), s32[]{:S(2)}) async-start(), calls=%async_computation.12 | async-start | bytes 7864320 | tf_op jit(solution)/shard_map/reduce_scatter | solution.py:287
  521.2 34.6 %collective-permute-start.38 = (bf16[128,2048]{1,0:T(8,128)(2,1)}, bf16[128,2048]{1,0:T(8,128)(2,1)S(1)}, u32[]{:S(2)}, u32[]{:S(2)}) collective-permute-start(bf16[128,2048]{1,0:T(8,128)(2,1)} %get-tuple-element.112), channel_id=1, source_target_pairs={{0,4},{4,0},{1,5},{5,1},{2,6},{6,2},{3,7},{7,3},{8,12},{12,8},{9,1... | collective-permute-start | bytes 1572872 | tf_op jit(solution)/shard_map/ppermute | solution.py:31
  521.7 34.0 %collective-permute-start.37 = (bf16[128,2048]{1,0:T(8,128)(2,1)}, bf16[128,2048]{1,0:T(8,128)(2,1)S(1)}, u32[]{:S(2)}, u32[]{:S(2)}) collective-permute-start(bf16[128,2048]{1,0:T(8,128)(2,1)} %get-tuple-element.110), channel_id=1, source_target_pairs={{0,1},{1,0},{2,3},{3,2},{4,5},{5,4},{6,7},{7,6},{8,9},{9,8},{10,11... | collective-permute-start | bytes 1572872 | tf_op jit(solution)/shard_map/ppermute | solution.py:35
  522.8 90.7 %collective-permute-start.46 = (bf16[384,1024]{1,0:T(8,128)(2,1)}, bf16[384,1024]{1,0:T(8,128)(2,1)S(1)}, u32[]{:S(2)}, u32[]{:S(2)}) collective-permute-start(bf16[384,1024]{1,0:T(8,128)(2,1)} %reduce-scatter.11.cloned.1.call-done), channel_id=1, source_target_pairs={{0,0},{8,1},{16,2},{24,3},{2,4},{10,5},{18,6},{26,7},{4,8},{12,9},... | collective-permute-start | bytes 2359304 | tf_op jit(solution)/shard_map/ppermute | solution.py:327
  574.4 83.5 %all-to-all-start.2 = ((bf16[4,128,768]{2,1,0:T(8,128)(2,1)}), bf16[4,128,768]{2,1,0:T(8,128)(2,1)S(1)}, u32[]{:S(2)}, u32[]{:S(2)}) async-start(bf16[4,128,768]{2,1,0:T(8,128)(2,1)} %bitcast.187), calls=%async_computation.3 | async-start | bytes 1572864 | tf_op jit(solution)/shard_map/all_to_all | solution.py:289
  615.8 42.1 %collective-permute-start.43 = (f32[16,272]{1,0:T(8,128)S(1)}, f32[16,272]{1,0:T(8,128)S(1)}, u32[]{:S(2)}, u32[]{:S(2)}) collective-permute-start(f32[16,272]{1,0:T(8,128)S(1)} %add.210), channel_id=1, source_target_pairs={{0,8},{8,0},{16,24},{24,16},{1,9},{9,1},{17,25},{25,17},{2,10},{10... | collective-permute-start | bytes 52232 | tf_op jit(solution)/shard_map/ppermute | solution.py:59
  657.9 80.6 %collective-permute-start.44 = (f32[16,272]{1,0:T(8,128)S(1)}, f32[16,272]{1,0:T(8,128)S(1)}, u32[]{:S(2)}, u32[]{:S(2)}) collective-permute-start(f32[16,272]{1,0:T(8,128)S(1)} %add.211), channel_id=1, source_target_pairs={{0,16},{8,24},{16,0},{24,8},{1,17},{9,25},{17,1},{25,9},{2,18},{10... | collective-permute-start | bytes 52232 | tf_op jit(solution)/shard_map/ppermute | solution.py:59
  (91 other events, 1531.5 us)
Sparse Core Ops, SparseCore 0:
  10.1 41.2 all-gather.10
  53.6 80.5 all-gather.6
  135.7 61.9 all-gather.12
  199.7 113.9 all-gather.8
  359.3 58.5 reduce-scatter.10
  479.5 94.8 reduce-scatter.4
  577.3 28.4 reduce-scatter.6
  608.1 124.0 reduce-scatter.8

commit v2 on v1

--- a/solution.py
+++ b/solution.py
@@ -9,12 +9,13 @@
 from jax.sharding import Mesh
 from jax.sharding import PartitionSpec as P
 
+
 f32 = jnp.float32
 bf16 = jnp.bfloat16
 eps_norm = 1e-06
 theta_base = 1000000.0
 masked_score = -1e30
-plane = ("x", "c", "y")
+data = ("h", "g")
 swap = [(0, 1), (1, 0)]
 cross = [(0, 3), (3, 0), (1, 2), (2, 1)]
 
@@ -27,57 +28,44 @@
     return lax.ppermute(v, "c", swap)
 
 
-def send_x(v):
-    return lax.ppermute(v, "x", swap)
-
-
-def send_y(v):
-    return lax.ppermute(v, "y", swap)
-
-
-def send_xy(v):
-    return lax.ppermute(v, ("x", "y"), cross)
-
-
-def gather_plane(v):
-    own = jnp.concatenate([v, send_y(v), send_x(v), send_xy(v)], axis=0)
-    return own, send_c(own)
-
-
-def reduce_plane(own, other):
-    total = own + send_c(other).astype(f32)
+def send_plane(y, x, xy):
+    return (
+        lax.ppermute(y, "y", swap),
+        lax.ppermute(x, "x", swap),
+        lax.ppermute(xy, ("x", "y"), cross),
+    )
+
+
+def send_mirror(v):
+    count = lax.axis_size("h") * lax.axis_size("g")
+    return lax.ppermute(v, data, [(i, count - 1 - i) for i in range(count)])
+
+
+def after(value, *others):
+    return lax.optimization_barrier((value, *others))[0]
+
+
+def gather_plane(v, *others):
+    own = jnp.concatenate([v, *send_plane(v, v, v)], axis=0)
+    return own, send_c(after(own, *others))
+
+
+def fold_cores(own, other):
+    theirs = send_c(other)
+    total = own + theirs.astype(f32)
     rows = own.shape[0] // 4
     part = [total[i * rows : (i + 1) * rows] for i in range(4)]
-    low = [p.astype(bf16) for p in part]
-    got = (send_y(low[1]), send_x(low[2]), send_xy(low[3]))
-    return part[0] + got[0].astype(f32) + got[1].astype(f32) + got[2].astype(f32)
-
-
-def doubling(v, axis, count, join):
-    step = 1
-    while step < count:
-        v = join(v, lax.ppermute(v, axis, [(i, i ^ step) for i in range(count)]), step)
-        step *= 2
-    return v
-
-
-def gather_rows(v, axis):
-    count = lax.axis_size(axis)
-    index = lax.axis_index(axis)
-
-    def join(mine, theirs, step):
-        low = (index & step) == 0
-        return jnp.where(
-            low,
-            jnp.concatenate([mine, theirs], axis=0),
-            jnp.concatenate([theirs, mine], axis=0),
-        )
-
-    return doubling(v, axis, count, join)
-
-
-def sum_all(v, axis):
-    return doubling(v, axis, lax.axis_size(axis), lambda a, b, step: a + b)
+    return part[0], [p.astype(bf16) for p in part[1:]]
+
+
+def finish(own, low):
+    got = send_plane(*low)
+    return own + got[0].astype(f32) + got[1].astype(f32) + got[2].astype(f32)
+
+
+def finish_pair(near, far):
+    moved = send_mirror(finish(*far).astype(bf16))
+    return finish(*near) + moved.astype(f32)
 
 
 def rms_scale(values):
@@ -195,7 +183,7 @@
     gain_out[0, 0, 1:2, :] = jnp.sum(addend, axis=0, keepdims=True)
 
 
-def rows_spec(micro, rows, width):
+def rows_spec(rows, width):
     return pl.BlockSpec((1, 2, 1, rows, width), lambda i, m: (i, 0, m, 0, 0))
 
 
@@ -203,7 +191,7 @@
     cos, sin, mask = tables
     rows, size = cos.shape[3], cos.shape[4]
     view = proj.reshape(2, 2, micro, rows, proj.shape[1])
-    spec = functools.partial(rows_spec, micro, rows)
+    spec = functools.partial(rows_spec, rows)
     out = pl.pallas_call(
         functools.partial(forward_kernel, size, group),
         grid=(2, micro),
@@ -224,7 +212,7 @@
 def attention_backward(proj, grad, tables, gains, group, micro):
     cos, sin, mask = tables
     rows, size = cos.shape[3], cos.shape[4]
-    spec = functools.partial(rows_spec, micro, rows)
+    spec = functools.partial(rows_spec, rows)
     out, sums = pl.pallas_call(
         functools.partial(backward_kernel, size, group),
         grid=(2, micro),
@@ -272,62 +260,103 @@
     return halves(cos), halves(sin), mask.astype(f32)
 
 
-def pack_columns(mats):
-    parts = [m.reshape(m.shape[0], 4, m.shape[1] // 4) for m in mats]
-    return jnp.concatenate(parts, axis=2).transpose(1, 0, 2)
-
-
-def share_columns(mats):
-    packed = lax.all_to_all(pack_columns(mats), ("x", "c"), split_axis=0, concat_axis=0, tiled=True)
-    packed = packed.reshape(packed.shape[0] * packed.shape[1], packed.shape[2])
-    return lax.all_gather(packed, "g", axis=0, tiled=True)
-
-
-def return_columns(grad, widths):
-    mine = lax.psum_scatter(grad, "g", scatter_dimension=0, tiled=True)
-    blocks = mine.reshape(4, mine.shape[0] // 4, mine.shape[1])
-    got = lax.all_to_all(blocks, ("x", "c"), split_axis=0, concat_axis=0, tiled=True)
-    outs, low = [], 0
-    for width in widths:
-        part = got[:, :, low : low + width].transpose(1, 0, 2)
-        outs.append(part.reshape(part.shape[0], 4 * width).astype(f32))
-        low += width
-    return outs
-
-
-def row_route(group_count, col_count):
-    per = group_count // col_count
+def pack_kernel(count, *refs):
+    *mats, out = refs
+    low = 0
+    for mat in mats:
+        wide = mat.shape[1] // count
+        for i in range(count):
+            out[0, i, :, low : low + wide] = mat[:, i * wide : (i + 1) * wide]
+        low += wide
+
+
+def pack_columns(mats, count, copies):
+    rows, width = mats[0].shape[0], sum(m.shape[1] for m in mats) // count
+    out = pl.pallas_call(
+        functools.partial(pack_kernel, count),
+        grid=(copies,),
+        in_specs=[pl.BlockSpec(m.shape, lambda i: (0, 0)) for m in mats],
+        out_specs=pl.BlockSpec((1, count, rows, width), lambda i: (i, 0, 0, 0)),
+        out_shape=jax.ShapeDtypeStruct((copies, count, rows, width), mats[0].dtype),
+        name="pack_columns",
+    )(*mats)
+    return out.reshape(copies * count, rows, width)
+
+
+def unpack_kernel(widths, got, *outs):
+    copies, count = got.shape[:2]
+    for i in range(count):
+        total = got[0, i].astype(f32)
+        for j in range(1, copies):
+            total = total + got[j, i].astype(f32)
+        low = 0
+        for width, out in zip(widths, outs):
+            out[:, i * width : (i + 1) * width] = total[:, low : low + width]
+            low += width
+
+
+def unpack_columns(got, count, widths):
+    copies, rows = got.shape[0] // count, got.shape[1]
+    step = min(rows, 32)
+    return pl.pallas_call(
+        functools.partial(unpack_kernel, widths),
+        grid=(rows // step,),
+        in_specs=[pl.BlockSpec((copies, count, step, got.shape[2]), lambda i: (0, 0, i, 0))],
+        out_specs=[pl.BlockSpec((step, count * w), lambda i: (i, 0)) for w in widths],
+        out_shape=[jax.ShapeDtypeStruct((rows, count * w), f32) for w in widths],
+        name="unpack_columns",
+    )(got.reshape(copies, count, rows, got.shape[2]))
+
+
+def exchange(blocks, axes):
+    return lax.all_to_all(blocks, axes, split_axis=0, concat_axis=0, tiled=True)
+
+
+def collect(mine, axes, axis):
+    return lax.all_gather(mine, axes, axis=axis, tiled=True)
+
+
+def scatter(full, axes, axis):
+    return lax.psum_scatter(full, axes, scatter_dimension=axis, tiled=True)
+
+
+def route_by(v, pairs):
+    return lax.ppermute(v, every, pairs)
+
+
+every = ("h", "g", "x", "c", "y")
+
+
+def row_route(ranks, fsdp_count, col_count):
+    per = fsdp_count // (ranks * col_count)
+    planes = fsdp_count // 4
     pairs = []
-    for f in range(4 * group_count):
+    for f in range(fsdp_count):
         for y in range(col_count):
             block, inner = f // per, f % per
-            target = inner * col_count + y
-            y_to, rest = block // 4, block % 4
-            pairs.append((f * col_count + y, (target * 4 + rest) * col_count + y_to))
+            y_to, rest = block // ranks, block % ranks
+            plane = inner * col_count + y + rest // 4 * (planes // 2)
+            pairs.append((f * col_count + y, (plane * 4 + rest % 4) * col_count + y_to))
     return pairs
 
 
-every = ("g", "x", "c", "y")
-
-
-def share_rows(mat, route, col_count):
-    moved = lax.ppermute(mat, every, route)
-    full = lax.all_gather(moved[None], "g", axis=0, tiled=True)
+def join_rows(full, col_count):
     count, rows, cols = full.shape
     full = full.reshape(count // col_count, col_count, rows, cols).transpose(0, 2, 1, 3)
     return full.reshape(count // col_count * rows, col_count * cols)
 
 
-def return_rows(grad, route, group_count, col_count):
-    per = group_count // col_count
-    rows, cols = grad.shape[0] // per, grad.shape[1] // col_count
-    blocks = grad.reshape(per, rows, col_count, cols).transpose(0, 2, 1, 3)
-    blocks = blocks.reshape(group_count * rows, cols)
-    mine = lax.psum_scatter(blocks, "g", scatter_dimension=0, tiled=True)
-    return lax.ppermute(mine, every, [(b, a) for a, b in route]).astype(f32)
-
-
-def body(
+def return_rows(grad, axes, route, col_count):
+    count = lax.axis_size(axes)
+    rows, cols = grad.shape[0] // (count // col_count), grad.shape[1] // col_count
+    blocks = [
+        grad[i // col_count * rows :, i % col_count * cols :][:rows, :cols] for i in range(count)
+    ]
+    mine = scatter(jnp.concatenate(blocks), axes, 0)
+    return route_by(mine, [(b, a) for a, b in route]).astype(f32)
+
+
+def inner_body(
     block_input,
     doc_lengths,
     norm_attn,
@@ -344,93 +373,158 @@
     w_down,
     grad_output,
 ):
-    group_count, col_count = lax.axis_size("g"), lax.axis_size("y")
-    fsdp_count = 4 * group_count
+    col_count = lax.axis_size("y")
+    fsdp_count = 4 * lax.axis_size(data)
     side = lax.axis_index("y")
-    owner = lax.axis_index("g") * 4 + lax.axis_index("x") * 2 + lax.axis_index("c")
     micro, _, rows, width = block_input.shape
     size = gain_query.shape[0] * fsdp_count
     group = w_query.shape[1] // w_key.shape[1]
-    route = row_route(group_count, col_count)
+    shards, near, wide = ("h", "g", "x", "c"), ("x", "c"), ("h", "x", "c")
+    plane_count = fsdp_count // 4
+    route_out = row_route(4, fsdp_count, col_count)
+    route_down = row_route(8, fsdp_count, col_count)
 
     tokens_low = block_input.reshape(micro * rows, width)
     cotangent = grad_output.reshape(micro * rows, width)
 
-    token_pair = gather_plane(tokens_low)
-    packed = jnp.concatenate([norm_attn, norm_ffn, gain_query, gain_key])[None]
-    every_gain = gather_rows(gather_rows(gather_rows(packed, "c"), "x"), "g").astype(f32)
+    flat = doc_lengths.reshape(-1)
+    packed = jnp.concatenate([norm_attn, norm_ffn, gain_query, gain_key, flat.astype(bf16)])
+    packed = jnp.broadcast_to(packed, (fsdp_count, packed.shape[0]))
+    every_gain = exchange(packed, shards).astype(f32)
+    every_length = every_gain[:, -flat.shape[0] :].astype(jnp.int32)
+    owner = lax.axis_index(shards)
     piece, small = norm_attn.shape[0], gain_query.shape[0]
     gain_one = every_gain[:, :piece].reshape(1, width)
     gain_two = every_gain[:, piece : 2 * piece].reshape(1, width)
     gain_q = every_gain[:, 2 * piece : 2 * piece + small].reshape(1, size)
-    gain_k = every_gain[:, 2 * piece + small :].reshape(1, size)
+    gain_k = every_gain[:, 2 * piece + small : 2 * piece + 2 * small].reshape(1, size)
     head_gains = jnp.concatenate([gain_q, gain_k], axis=0)
-    lengths = doc_lengths.reshape(1, micro, doc_lengths.shape[2])
-    lengths = jnp.concatenate([lengths, send_x(lengths)], axis=0)
-    tables = [make_tables(v, side, rows, size) for v in (lengths, send_c(lengths))]
-
-    qkvg = share_columns((w_query, w_key, w_value, w_gate_attn))
-    out_rows = share_rows(w_out, route, col_count)
-    gate_up = share_columns((w_gate, w_up))
-    down_rows = share_rows(w_down, route, col_count)
-    cot_pair = gather_plane(cotangent)
+
+    def lengths_of(core):
+        picked = [every_length[owner ^ core], every_length[owner ^ core ^ 2]]
+        return jnp.stack(picked).reshape(2, micro, doc_lengths.shape[2])
+
+    tables = [make_tables(lengths_of(core), side, rows, size) for core in (0, 1)]
+
+    packed_wide = pack_columns((w_gate, w_up), 8, 1)
+    packed = pack_columns((w_query, w_key, w_value, w_gate_attn), 4, 1)
+    moved = route_by(w_out, route_out)
+    spread = exchange(packed, near)
+    cut = moved.shape[1] // 4
+    moved = jnp.stack([moved[:, i * cut : (i + 1) * cut] for i in range(4)])
+    if moved.shape[1] == spread.shape[1]:
+        full = collect(jnp.concatenate([spread, moved], axis=2), data, 0)
+        full = full.reshape(plane_count, 4, *full.shape[1:])
+        qkvg, full = full[..., : spread.shape[2]], full[..., spread.shape[2] :]
+    else:
+        qkvg = collect(spread, data, 0)
+        full = collect(moved[None], data, 0)
+    qkvg = qkvg.reshape(width, spread.shape[2])
+    full = full.reshape(plane_count // col_count, col_count, 4, moved.shape[1], cut)
+    out_rows = full.transpose(0, 3, 1, 2, 4).reshape(-1, col_count * 4 * cut)
+    token_pair = gather_plane(after(tokens_low, spread), packed_wide)
+    cot_list = gather_plane(after(cotangent, token_pair[0]))
+    moved = route_by(after(w_down, token_pair[0]), route_down)
+    down_rows = join_rows(collect(moved[None], "g", 0), col_count)
+    far = send_mirror(after(cotangent, token_pair[0]))
+    cot_list += gather_plane(after(far, cot_list[0]))
+    spread = exchange(after(packed_wide, cot_list[0], far), wide)
+    gate_up = collect(spread.reshape(2, -1, spread.shape[2]), "g", 1)
+    gate_up = gate_up.reshape(-1, spread.shape[2])
 
     def first_norm(v):
         v = v.astype(f32)
         return (v * rms_scale(v) * gain_one).astype(bf16)
 
-    hidden = [first_norm(v) for v in token_pair]
-    proj = [dot(h, qkvg, 1, 0) for h in hidden]
-    gated = [attention_forward(p, t, head_gains, group, micro) for p, t in zip(proj, tables)]
-    mixed = reduce_plane(dot(gated[0], out_rows, 1, 0), dot(gated[1], out_rows, 1, 0, bf16))
+    def first_part(v, table):
+        h = first_norm(v)
+        p = dot(h, qkvg, 1, 0)
+        return h, p, attention_forward(p, table, head_gains, group, micro)
+
+    other = first_part(token_pair[1], tables[1])
+    mine = first_part(after(token_pair[0], other[2]), tables[0])
+    hidden, proj, gated = zip(mine, other)
+    mixed = fold_cores(dot(gated[0], out_rows, 1, 0), dot(gated[1], out_rows, 1, 0, bf16))
+    mixed = finish(*mixed)
     tokens = tokens_low.astype(f32)
     residual = tokens + mixed
     scale_two = rms_scale(residual)
-    hidden_two = gather_plane((residual * scale_two * gain_two).astype(bf16))
+    low = (residual * scale_two * gain_two).astype(bf16)
+    far = send_mirror(low)
+    hidden_two = gather_plane(low)
+    hidden_two += gather_plane(after(far, hidden_two[0]))
     units = gate_up.shape[1] // 2
 
     inner, grad_units = [], []
-    for h, g in zip(hidden_two, cot_pair):
+
+    def feed(h, g):
         pre = dot(h, gate_up, 1, 0)
         gate_pre, up_pre = pre[:, :units], pre[:, units:]
         grad_inner = dot(g, down_rows, 1, 1)
         sig = jax.nn.sigmoid(gate_pre)
         act = gate_pre * sig
-        inner.append((act * up_pre).astype(bf16))
+        zz = (act * up_pre).astype(bf16)
         grad_gate = grad_inner * up_pre * (sig * (1.0 + gate_pre * (1.0 - sig)))
-        grad_units.append(
-            jnp.concatenate([grad_gate.astype(bf16), (grad_inner * act).astype(bf16)], axis=1)
-        )
-    grad_hidden_two = reduce_plane(
-        dot(grad_units[0], gate_up, 1, 1), dot(grad_units[1], gate_up, 1, 1, bf16)
-    )
-    final = reduce_plane(dot(inner[0], down_rows, 1, 0), dot(inner[1], down_rows, 1, 0, bf16))
-    block_output = (residual + final).astype(bf16).reshape(block_input.shape)
+        pair = [grad_gate.astype(bf16), (grad_inner * act).astype(bf16)]
+        return zz, jnp.concatenate(pair, axis=1)
+
+    for i in range(4):
+        zz, pair = feed(hidden_two[i], cot_list[i])
+        inner.append(zz)
+        grad_units.append(pair)
+
+    def products(left, right, dim):
+        kinds = (f32, bf16, f32, bf16)
+        parts = [dot(v, right, 1, dim, kind) for v, kind in zip(left, kinds)]
+        return parts[:2], parts[2:]
 
     def weight_grad(left, right):
-        return (dot(left[0], right[0], 0, 0) + dot(left[1], right[1], 0, 0)).astype(bf16)
-
-    grad_down = return_rows(weight_grad(inner, cot_pair), route, group_count, col_count)
-    grad_gate, grad_up = return_columns(
-        weight_grad(hidden_two, grad_units), (units, units)
-    )
+        total = dot(left[0], right[0], 0, 0)
+        for a, b in zip(left[1:], right[1:]):
+            total = total + dot(a, b, 0, 0)
+        return total.astype(bf16)
+
+    near_parts, far_parts = products(grad_units, gate_up, 1)
+    far_parts, near_parts = fold_cores(*far_parts), fold_cores(*near_parts)
+    held = lax.optimization_barrier((*inner, *grad_units, *near_parts[1], *far_parts[1]))
+    held_inner, held_units = held[:4], held[4:8]
+    sum_units = weight_grad(hidden_two, held_units)
+    mine = scatter(sum_units.reshape(2, width // 2, 2 * units), "g", 1)
+    final_parts = products(held_inner, down_rows, 0)
+    held = lax.optimization_barrier((*final_parts[0], *final_parts[1]))
+    final_parts = fold_cores(*held[:2]), fold_cores(*held[2:])
+    sum_down = weight_grad(held_inner, cot_list)
+    grad_hidden_two = after(finish_pair(near_parts, far_parts), sum_down, sum_units)
 
     back, addend = norm_back(grad_hidden_two, residual, scale_two, gain_two)
     sum_two = jnp.sum(addend, axis=0)
     grad_resid = cotangent.astype(f32) + back
-    low_pair = gather_plane(grad_resid.astype(bf16))
-    grad_gated = [dot(d, out_rows, 1, 1) for d in low_pair]
-    backs = [
-        attention_backward(p, d, t, head_gains, group, micro)
-        for p, d, t in zip(proj, grad_gated, tables)
-    ]
+    low = grad_resid.astype(bf16)
+    low_pair = gather_plane(low)
+    got = exchange(mine.reshape(8, mine.shape[1] // 4, mine.shape[2]), wide)
+    grad_gate, grad_up = unpack_columns(got, 8, (units, units))
+    grad_down = return_rows(sum_down, "g", route_down, col_count)
+    sum_out = weight_grad(gated, low_pair)
+    grad_out = return_rows(sum_out, data, route_out, col_count)
+    held = lax.optimization_barrier((*low_pair, sum_out))[:2]
+    final = finish_pair(*final_parts)
+    block_output = (residual + final).astype(bf16).reshape(block_input.shape)
+    grad_gated = [dot(d, out_rows, 1, 1) for d in held]
+
+    def attention_part(i):
+        return attention_backward(proj[i], grad_gated[i], tables[i], head_gains, group, micro)
+
+    backs = [attention_part(0), attention_part(1)]
     grad_proj = [b[0] for b in backs]
-    grad_hidden = reduce_plane(dot(grad_proj[0], qkvg, 1, 1), dot(grad_proj[1], qkvg, 1, 1, bf16))
-    grad_out = return_rows(weight_grad(gated, low_pair), route, group_count, col_count)
+    sum_proj = weight_grad(hidden, grad_proj)
+    got = exchange(sum_proj.reshape(fsdp_count, -1, sum_proj.shape[1]), shards)
     query_width, key_width = group * size, size
-    grad_query, grad_key, grad_value, grad_gate_attn = return_columns(
-        weight_grad(hidden, grad_proj), (query_width, key_width, key_width, query_width)
+    grad_query, grad_key, grad_value, grad_gate_attn = unpack_columns(
+        got, 4, (query_width, key_width, key_width, query_width)
     )
+    grad_proj = lax.optimization_barrier((*grad_proj, sum_proj, block_output))[:2]
+    parts = dot(grad_proj[0], qkvg, 1, 1), dot(grad_proj[1], qkvg, 1, 1, bf16)
+    grad_hidden = finish(*fold_cores(*parts))
     back, addend = norm_back(grad_hidden, tokens, rms_scale(tokens), gain_one)
     grad_input = (grad_resid + back).reshape(block_input.shape)
 
@@ -444,9 +538,8 @@
         ],
         axis=1,
     )
-    for axis in ("c", "y", "x", "g"):
-        sums = sum_all(sums, axis)
-    mine = lax.dynamic_index_in_dim(sums, owner, 0, keepdims=False)
+    mine = jnp.sum(exchange(after(sums, got), shards), axis=0)
+    mine = mine + lax.ppermute(mine, "y", swap)
     return (
         block_output,
         grad_input,
@@ -467,8 +560,8 @@
 
 def solution(mesh):
     fsdp_count, col_count = mesh.shape["fsdp"], mesh.shape["col"]
-    grid = Mesh(mesh.devices.reshape(fsdp_count // 4, 2, 2, col_count), every)
-    rows = ("g", "x", "c")
+    grid = Mesh(mesh.devices.reshape(2, fsdp_count // 8, 2, 2, col_count), every)
+    rows = ("h", "g", "x", "c")
     token, vector, matrix = P(None, rows, "y", None), P(rows), P(rows, "y")
     in_specs = (
         (token, P(None, rows, None), vector)
@@ -478,4 +571,4 @@
         + (token,)
     )
     out_specs = (token, token, vector) + (matrix,) * 5 + (vector,) * 3 + (matrix,) * 3
-    return jax.shard_map(body, mesh=grid, in_specs=in_specs, out_specs=out_specs, check_vma=False)
+    return jax.shard_map(inner_body, mesh=grid, in_specs=in_specs, out_specs=out_specs, check_vma=False)

time: 774 us -> 756 us (0.977)
  the two profiles are of different devices: /device:TPU:0 before, /device:TPU:1 now
where the time goes in v2:
time: 756 us; the launch traced here: 745 us
  waiting for transfers between devices  345 us (46%)
  starting transfers between devices  130 us (17%)
  matrix products  127 us (17%)
  other arithmetic  44.1 us (6%)
  Pallas kernels  42.7 us (6%)
  local copies, waits for them, and re-layouts  39.6 us (5%)
  between operations  16.9 us (2%)
    dot_general x36, matrix products, dot(): lax.dot_general(a, b, (((ca,), (cb,)), ((), ())), preferred_element_type=...  127 us
    ppermute x12, waiting for transfers between devices, send_plane(): lax.ppermute(xy, ('x', 'y'), cross)  84 us
    ppermute x4, waiting for transfers between devices, route_by(): return lax.ppermute(v, every, pairs)  74 us
    ppermute x12, waiting for transfers between devices, send_plane(): lax.ppermute(x, 'x', swap)  57 us
    all_to_all x6, starting transfers between devices, exchange(): return lax.all_to_all(blocks, axes, split_axis=0, concat_axis=0, tiled=True)  41.4 us
    all_to_all x6, waiting for transfers between devices, exchange(): return lax.all_to_all(blocks, axes, split_axis=0, concat_axis=0, tiled=True)  35.2 us
    all_gather x3, waiting for transfers between devices, collect(): return lax.all_gather(mine, axes, axis=axis, tiled=True)  32.8 us
    ppermute x12, waiting for transfers between devices, send_plane(): lax.ppermute(y, 'y', swap)  25.9 us
  transfers between devices with their start and end apart: 69, of which 31 were waited for; matrix products, arithmetic and copies ran while one was open for 26% of the time, Pallas kernels for 5%

profile of v2, /device:TPU:1, one launch (start us, length us, event | category | flops | bytes accessed | tf_op | source)
XLA Modules:
  0.0 745.3 jit_solution(17307359604297969908)
XLA Ops:
  19.4 11.6 %collective-permute-done.4 = bf16[128,1024]{1,0:T(8,128)(2,1)S(1)} collective-permute-done((bf16[128,1024]{1,0:T(8,128)(2,1)S(1)}, bf16[128,1024]{1,0:T(8,128)(2,1)S(1)}, u32[]{:S(2)}, u32[]{:S(2)}) %collective-permute-start.4) | collective-permute-done | bytes 262176 | tf_op jit(solution)/shard_map/ppermute | solution.py:324
  50.1 9.4 %collective-permute-done = bf16[128,2048]{1,0:T(8,128)(2,1)S(1)} collective-permute-done((bf16[128,2048]{1,0:T(8,128)(2,1)S(1)}, bf16[128,2048]{1,0:T(8,128)(2,1)S(1)}, u32[]{:S(2)}, u32[]{:S(2)}) %collective-permute-start) | collective-permute-done | bytes 524320 | tf_op jit(solution)/shard_map/ppermute | solution.py:33
  61.6 10.2 %collective-permute-done.2 = bf16[128,2048]{1,0:T(8,128)(2,1)S(1)} collective-permute-done((bf16[128,2048]{1,0:T(8,128)(2,1)S(1)}, bf16[128,2048]{1,0:T(8,128)(2,1)S(1)}, u32[]{:S(2)}, u32[]{:S(2)}) %collective-permute-start.2) | collective-permute-done | bytes 524320 | tf_op jit(solution)/shard_map/ppermute | solution.py:35
  84.9 7.9 %collective-permute-done.12 = bf16[128,2048]{1,0:T(8,128)(2,1)S(1)} collective-permute-done((bf16[128,2048]{1,0:T(8,128)(2,1)S(1)}, bf16[128,2048]{1,0:T(8,128)(2,1)S(1)}, u32[]{:S(2)}, u32[]{:S(2)}) %collective-permute-start.12) | collective-permute-done | bytes 524320 | tf_op jit(solution)/shard_map/ppermute | solution.py:33
  105.4 32.8 %all-gather.5.cloned.1.call-done = bf16[16,128,1024]{2,1,0:T(8,128)(2,1)} async-done(((bf16[4,128,1024]{2,1,0:T(8,128)(2,1)}), bf16[16,128,1024]{2,1,0:T(8,128)(2,1)}) %all-gather.5.cloned.1.call-update) | async-done | bytes 4194320 | tf_op jit(solution)/shard_map/all_gather | solution.py:316
  187.4 14.4 %all-to-all-done.2 = bf16[8,128,768]{2,1,0:T(8,128)(2,1)} async-done(((bf16[8,128,768]{2,1,0:T(8,128)(2,1)}), bf16[8,128,768]{2,1,0:T(8,128)(2,1)}, u32[]{:S(2)}, u32[]{:S(2)}) %all-to-all-start.2) | async-done | bytes 1572896 | tf_op jit(solution)/shard_map/all_to_all | solution.py:312
  205.4 10.8 %collective-permute-done.7 = bf16[128,2048]{1,0:T(8,128)(2,1)S(1)} collective-permute-done((bf16[128,2048]{1,0:T(8,128)(2,1)S(1)}, bf16[128,2048]{1,0:T(8,128)(2,1)S(1)}, u32[]{:S(2)}, u32[]{:S(2)}) %collective-permute-start.7) | collective-permute-done | bytes 524320 | tf_op jit(solution)/shard_map/ppermute | solution.py:34
  222.0 11.6 %collective-permute-start.17 = (bf16[128,2048]{1,0:T(8,128)(2,1)S(1)}, bf16[128,2048]{1,0:T(8,128)(2,1)}, u32[]{:S(2)}, u32[]{:S(2)}) collective-permute-start(bf16[128,2048]{1,0:T(8,128)(2,1)S(1)} %multiply_convert_fusion), channel_id=1, source_target_pairs={{0,24},{8,16},{16,8},{24,0},{1,25},{9,17},{17,9},{25,1},{2,26},{10... | collective-permute-start | bytes 1572872 | tf_op jit(solution)/shard_map/ppermute | solution.py:41
  247.2 9.8 %collective-permute-done.17 = bf16[128,2048]{1,0:T(8,128)(2,1)} collective-permute-done((bf16[128,2048]{1,0:T(8,128)(2,1)S(1)}, bf16[128,2048]{1,0:T(8,128)(2,1)}, u32[]{:S(2)}, u32[]{:S(2)}) %collective-permute-start.17) | collective-permute-done | bytes 524320 | tf_op jit(solution)/shard_map/ppermute | solution.py:41
  369.8 7.8 %add_convert_fusion.1 = bf16[2048,768]{1,0:T(8,128)(2,1)} fusion(f32[2048,768]{1,0:T(8,128)S(1)} %fusion.81, f32[2048,768]{1,0:T(8,128)} %fusion.49, f32[2048,768]{1,0:T(8,128)S(1)} %fusion.80, bf16[512,2048]{1,0:T(8,128)(2,1)} %collective-permute-done.21, bf16[512,768]{1,0:T(8,128)(2,1)S(1)} %copy-done.15), kind=kOutput, calls=%fused_computation.1 | convolution fusion | flops 1616904192 | bytes 24903680 | tf_op jit(solution)/shard_map/dot_general | solution.py:24
  395.8 24.3 %collective-permute-done.37 = bf16[128,2048]{1,0:T(8,128)(2,1)S(1)} collective-permute-done((bf16[128,2048]{1,0:T(8,128)(2,1)S(1)}, bf16[128,2048]{1,0:T(8,128)(2,1)S(1)}, u32[]{:S(2)}, u32[]{:S(2)}) %collective-permute-start.37) | collective-permute-done | bytes 524320 | tf_op jit(solution)/shard_map/ppermute | solution.py:35
  420.9 10.0 %collective-permute-done.36 = bf16[128,2048]{1,0:T(8,128)(2,1)S(1)} collective-permute-done((bf16[128,2048]{1,0:T(8,128)(2,1)S(1)}, bf16[128,2048]{1,0:T(8,128)(2,1)S(1)}, u32[]{:S(2)}, u32[]{:S(2)}) %collective-permute-start.36) | collective-permute-done | bytes 524320 | tf_op jit(solution)/shard_map/ppermute | solution.py:34
  437.3 7.7 %collective-permute-done.45 = bf16[128,2048]{1,0:T(8,128)(2,1)S(1)} collective-permute-done((bf16[128,2048]{1,0:T(8,128)(2,1)S(1)}, bf16[128,2048]{1,0:T(8,128)(2,1)S(1)}, u32[]{:S(2)}, u32[]{:S(2)}) %collective-permute-start.45) | collective-permute-done | bytes 524320 | tf_op jit(solution)/shard_map/ppermute | solution.py:41
  446.9 7.8 %collective-permute-done.32 = bf16[128,2048]{1,0:T(8,128)(2,1)S(1)} collective-permute-done((bf16[128,2048]{1,0:T(8,128)(2,1)S(1)}, bf16[128,2048]{1,0:T(8,128)(2,1)S(1)}, u32[]{:S(2)}, u32[]{:S(2)}) %collective-permute-start.32) | collective-permute-done | bytes 524320 | tf_op jit(solution)/shard_map/ppermute | solution.py:34
  461.6 10.3 %collective-permute-done.48 = bf16[128,2048]{1,0:T(8,128)(2,1)S(1)} collective-permute-done((bf16[128,2048]{1,0:T(8,128)(2,1)S(1)}, bf16[128,2048]{1,0:T(8,128)(2,1)S(1)}, u32[]{:S(2)}, u32[]{:S(2)}) %collective-permute-start.48) | collective-permute-done | bytes 524320 | tf_op jit(solution)/shard_map/ppermute | solution.py:35
  471.9 10.7 %collective-permute-done.47 = bf16[128,2048]{1,0:T(8,128)(2,1)S(1)} collective-permute-done((bf16[128,2048]{1,0:T(8,128)(2,1)S(1)}, bf16[128,2048]{1,0:T(8,128)(2,1)S(1)}, u32[]{:S(2)}, u32[]{:S(2)}) %collective-permute-start.47) | collective-permute-done | bytes 524320 | tf_op jit(solution)/shard_map/ppermute | solution.py:34
  498.8 8.9 %attn_bwd.2 = (bf16[2,2,2,64,768]{4,3,2,1,0:T(8,128)(2,1)}, f32[2,2,2,128]{3,2,1,0:T(2,128)}) custom-call(f32[2,2,2,64,768]{4,3,2,1,0:T(8,128)} %fusion.71.proj, f32[2,2,2,64,256]{4,3,2,1,0:T(8,128)} %fusion.34.grad, f32[2,2,2,64,128]{4,3,2,1,0:T(8,128)} %maximum_bitcast_fusion.2.cos, f32[2,2,2,64,128]{4,3,2,1,0:T(8,128)} %maximum_bitcast_fusion.3.sin, ...), custom_call_target="tpu_custom_call" | custom-call | tf_op jit(solution)/shard_map/attn_bwd/pallas_call | solution.py:216
  511.0 9.0 %attn_bwd.3 = (bf16[2,2,2,64,768]{4,3,2,1,0:T(8,128)(2,1)}, f32[2,2,2,128]{3,2,1,0:T(2,128)}) custom-call(f32[2,2,2,64,768]{4,3,2,1,0:T(8,128)} %fusion.70.proj, f32[2,2,2,64,256]{4,3,2,1,0:T(8,128)} %fusion.32.grad, f32[2,2,2,64,128]{4,3,2,1,0:T(8,128)} %maximum_bitcast_fusion.cos, f32[2,2,2,64,128]{4,3,2,1,0:T(8,128)} %maximum_bitcast_fusion.1.sin, ...), custom_call_target="tpu_custom_call" | custom-call | tf_op jit(solution)/shard_map/attn_bwd/pallas_call | solution.py:216
  526.9 18.7 %all-to-all-start.3 = ((bf16[16,128,768]{2,1,0:T(8,128)(2,1)}), bf16[16,128,768]{2,1,0:T(8,128)(2,1)}, u32[]{:S(2)}, u32[]{:S(2)}) async-start(bf16[16,128,768]{2,1,0:T(8,128)(2,1)} %bitcast.40), calls=%async_computation.3 | async-start | bytes 6291456 | tf_op jit(solution)/shard_map/all_to_all | solution.py:312
  567.0 24.0 %collective-permute-done.53 = bf16[128,2048]{1,0:T(8,128)(2,1)S(1)} collective-permute-done((bf16[128,2048]{1,0:T(8,128)(2,1)}, bf16[128,2048]{1,0:T(8,128)(2,1)S(1)}, u32[]{:S(2)}, u32[]{:S(2)}) %collective-permute-start.53) | collective-permute-done | bytes 524320 | tf_op jit(solution)/shard_map/ppermute | solution.py:35
  591.0 12.6 %collective-permute-done.52 = bf16[128,2048]{1,0:T(8,128)(2,1)S(1)} collective-permute-done((bf16[128,2048]{1,0:T(8,128)(2,1)}, bf16[128,2048]{1,0:T(8,128)(2,1)S(1)}, u32[]{:S(2)}, u32[]{:S(2)}) %collective-permute-start.52) | collective-permute-done | bytes 524320 | tf_op jit(solution)/shard_map/ppermute | solution.py:34
  606.3 11.9 %all-to-all-done.3 = bf16[16,128,768]{2,1,0:T(8,128)(2,1)} async-done(((bf16[16,128,768]{2,1,0:T(8,128)(2,1)}), bf16[16,128,768]{2,1,0:T(8,128)(2,1)}, u32[]{:S(2)}, u32[]{:S(2)}) %all-to-all-start.3) | async-done | bytes 3145760 | tf_op jit(solution)/shard_map/all_to_all | solution.py:312
  641.0 12.7 %reduce-scatter.4.cloned.1.call-done = bf16[128,1024]{1,0:T(8,128)(2,1)} async-done(((bf16[512,1024]{1,0:T(8,128)(2,1)}), bf16[128,1024]{1,0:T(8,128)(2,1)}) %reduce-scatter.4.cloned.1.call-update) | async-done | bytes 262160 | tf_op jit(solution)/shard_map/reduce_scatter | solution.py:320
  661.3 62.4 %collective-permute-done.55 = bf16[128,1024]{1,0:T(8,128)(2,1)S(1)} collective-permute-done((bf16[128,1024]{1,0:T(8,128)(2,1)}, bf16[128,1024]{1,0:T(8,128)(2,1)S(1)}, u32[]{:S(2)}, u32[]{:S(2)}) %collective-permute-start.55) | collective-permute-done | bytes 262176 | tf_op jit(solution)/shard_map/ppermute | solution.py:324
  (381 shorter events, 371.3 us)
Async XLA Ops:
  14.5 123.8 %all-gather.5.cloned.1.call-start = ((), (), s32[]{:S(2)}) async-start(), calls=%async_computation.9 | async-start | bytes 5242880 | tf_op jit(solution)/shard_map/all_gather | solution.py:316
  82.3 74.6 %collective-permute-start.13 = (bf16[128,2048]{1,0:T(8,128)(2,1)S(1)}, bf16[128,2048]{1,0:T(8,128)(2,1)}, u32[]{:S(2)}, u32[]{:S(2)}) collective-permute-start(bf16[128,2048]{1,0:T(8,128)(2,1)S(1)} %bitcast.169), channel_id=1, source_target_pairs={{0,4},{4,0},{1,5},{5,1},{2,6},{6,2},{3,7},{7,3},{8,12},{12,8},{9,1... | collective-permute-start | bytes 1572872 | tf_op jit(solution)/shard_map/ppermute | solution.py:34
  82.8 76.0 %collective-permute-start.14 = (bf16[128,2048]{1,0:T(8,128)(2,1)S(1)}, bf16[128,2048]{1,0:T(8,128)(2,1)}, u32[]{:S(2)}, u32[]{:S(2)}) collective-permute-start(bf16[128,2048]{1,0:T(8,128)(2,1)S(1)} %bitcast.170), channel_id=1, source_target_pairs={{0,5},{5,0},{1,4},{4,1},{2,7},{7,2},{3,6},{6,3},{8,13},{13,8},{9,1... | collective-permute-start | bytes 1572872 | tf_op jit(solution)/shard_map/ppermute | solution.py:35
  83.5 77.2 %collective-permute-start.15 = (bf16[128,2048]{1,0:T(8,128)(2,1)S(1)}, bf16[128,2048]{1,0:T(8,128)(2,1)}, u32[]{:S(2)}, u32[]{:S(2)}) collective-permute-start(bf16[128,2048]{1,0:T(8,128)(2,1)S(1)} %bitcast.171), channel_id=1, source_target_pairs={{0,24},{8,16},{16,8},{24,0},{1,25},{9,17},{17,9},{25,1},{2,26},{10... | collective-permute-start | bytes 1572872 | tf_op jit(solution)/shard_map/ppermute | solution.py:41
  92.8 72.7 %collective-permute-start.22 = (bf16[384,1024]{1,0:T(8,128)(2,1)}, bf16[384,1024]{1,0:T(8,128)(2,1)}, u32[]{:S(2)}, u32[]{:S(2)}) collective-permute-start(bf16[384,1024]{1,0:T(8,128)(2,1)} %param.28), channel_id=1, source_target_pairs={{0,0},{1,8},{2,2},{3,10},{4,4},{5,12},{6,6},{7,14},{8,16},{9,24},{... | collective-permute-start | bytes 2359304 | tf_op jit(solution)/shard_map/ppermute | solution.py:324
  160.7 41.1 %all-to-all-start.2 = ((bf16[8,128,768]{2,1,0:T(8,128)(2,1)}), bf16[8,128,768]{2,1,0:T(8,128)(2,1)}, u32[]{:S(2)}, u32[]{:S(2)}) async-start(bf16[8,128,768]{2,1,0:T(8,128)(2,1)} %bitcast.156), calls=%async_computation.2 | async-start | bytes 3145728 | tf_op jit(solution)/shard_map/all_to_all | solution.py:312
  165.6 101.2 %all-gather.9.cloned.1.call-start = ((), (), s32[]{:S(2)}) async-start(), calls=%async_computation.14 | async-start | bytes 2359296 | tf_op jit(solution)/shard_map/all_gather | solution.py:316
  166.1 124.6 %all-gather.7.cloned.1.call-start = ((), (), s32[]{:S(2)}) async-start(), calls=%async_computation.10 | async-start | bytes 4718592 | tf_op jit(solution)/shard_map/all_gather | solution.py:316
  201.8 421.3 %reduce-scatter.6.cloned.1.call-start = ((), (), s32[]{:S(2)}) async-start(), calls=%async_computation.12 | async-start | bytes 4718592 | tf_op jit(solution)/shard_map/reduce_scatter | solution.py:320
  243.0 58.8 %collective-permute-start.23 = (bf16[512,2048]{1,0:T(8,128)(2,1)}, bf16[512,2048]{1,0:T(8,128)(2,1)}, u32[]{:S(2)}, u32[]{:S(2)}) collective-permute-start(bf16[512,2048]{1,0:T(8,128)(2,1)} %constant_dynamic-update-slice_fusion.4), channel_id=1, source_target_pairs={{0,2},{2,0},{1,3},{3,1},{4,6},{6,4},{5,7},{7,5},{8,10},{10,8},{9,1... | collective-permute-start | bytes 6291464 | tf_op jit(solution)/shard_map/ppermute | solution.py:28
  333.5 50.2 %collective-permute-start.44 = (bf16[128,2048]{1,0:T(8,128)(2,1)}, bf16[128,2048]{1,0:T(8,128)(2,1)}, u32[]{:S(2)}, u32[]{:S(2)}) collective-permute-start(bf16[128,2048]{1,0:T(8,128)(2,1)} %get-tuple-element.198), channel_id=1, source_target_pairs={{0,5},{5,0},{1,4},{4,1},{2,7},{7,2},{3,6},{6,3},{8,13},{13,8},{9,1... | collective-permute-start | bytes 1572872 | tf_op jit(solution)/shard_map/ppermute | solution.py:35
  334.9 50.2 %collective-permute-start.43 = (bf16[128,2048]{1,0:T(8,128)(2,1)}, bf16[128,2048]{1,0:T(8,128)(2,1)}, u32[]{:S(2)}, u32[]{:S(2)}) collective-permute-start(bf16[128,2048]{1,0:T(8,128)(2,1)} %get-tuple-element.199), channel_id=1, source_target_pairs={{0,4},{4,0},{1,5},{5,1},{2,6},{6,2},{3,7},{7,3},{8,12},{12,8},{9,1... | collective-permute-start | bytes 1572872 | tf_op jit(solution)/shard_map/ppermute | solution.py:34
  335.5 50.2 %collective-permute-start.42 = (bf16[128,2048]{1,0:T(8,128)(2,1)}, bf16[128,2048]{1,0:T(8,128)(2,1)}, u32[]{:S(2)}, u32[]{:S(2)}) collective-permute-start(bf16[128,2048]{1,0:T(8,128)(2,1)} %get-tuple-element.200), channel_id=1, source_target_pairs={{0,1},{1,0},{2,3},{3,2},{4,5},{5,4},{6,7},{7,6},{8,9},{9,8},{10,11... | collective-permute-start | bytes 1572872 | tf_op jit(solution)/shard_map/ppermute | solution.py:33
  383.7 49.1 %collective-permute-start.41 = (bf16[128,2048]{1,0:T(8,128)(2,1)S(1)}, bf16[128,2048]{1,0:T(8,128)(2,1)S(1)}, u32[]{:S(2)}, u32[]{:S(2)}) collective-permute-start(bf16[128,2048]{1,0:T(8,128)(2,1)S(1)} %copy-done.29), channel_id=1, source_target_pairs={{0,5},{5,0},{1,4},{4,1},{2,7},{7,2},{3,6},{6,3},{8,13},{13,8},{9,1... | collective-permute-start | bytes 1572872 | tf_op jit(solution)/shard_map/ppermute | solution.py:35
  385.1 48.1 %collective-permute-start.40 = (bf16[128,2048]{1,0:T(8,128)(2,1)S(1)}, bf16[128,2048]{1,0:T(8,128)(2,1)S(1)}, u32[]{:S(2)}, u32[]{:S(2)}) collective-permute-start(bf16[128,2048]{1,0:T(8,128)(2,1)S(1)} %copy-done.28), channel_id=1, source_target_pairs={{0,4},{4,0},{1,5},{5,1},{2,6},{6,2},{3,7},{7,3},{8,12},{12,8},{9,1... | collective-permute-start | bytes 1572872 | tf_op jit(solution)/shard_map/ppermute | solution.py:34
  391.9 39.1 %collective-permute-start.36 = (bf16[128,2048]{1,0:T(8,128)(2,1)S(1)}, bf16[128,2048]{1,0:T(8,128)(2,1)S(1)}, u32[]{:S(2)}, u32[]{:S(2)}) collective-permute-start(bf16[128,2048]{1,0:T(8,128)(2,1)S(1)} %get-tuple-element.197), channel_id=1, source_target_pairs={{0,4},{4,0},{1,5},{5,1},{2,6},{6,2},{3,7},{7,3},{8,12},{12,8},{9,1... | collective-permute-start | bytes 1572872 | tf_op jit(solution)/shard_map/ppermute | solution.py:34
  392.3 38.7 %collective-permute-start.35 = (bf16[128,2048]{1,0:T(8,128)(2,1)S(1)}, bf16[128,2048]{1,0:T(8,128)(2,1)S(1)}, u32[]{:S(2)}, u32[]{:S(2)}) collective-permute-start(bf16[128,2048]{1,0:T(8,128)(2,1)S(1)} %get-tuple-element.195), channel_id=1, source_target_pairs={{0,1},{1,0},{2,3},{3,2},{4,5},{5,4},{6,7},{7,6},{8,9},{9,8},{10,11... | collective-permute-start | bytes 1572872 | tf_op jit(solution)/shard_map/ppermute | solution.py:33
  526.9 91.3 %all-to-all-start.3 = ((bf16[16,128,768]{2,1,0:T(8,128)(2,1)}), bf16[16,128,768]{2,1,0:T(8,128)(2,1)}, u32[]{:S(2)}, u32[]{:S(2)}) async-start(bf16[16,128,768]{2,1,0:T(8,128)(2,1)} %bitcast.40), calls=%async_computation.3 | async-start | bytes 6291456 | tf_op jit(solution)/shard_map/all_to_all | solution.py:312
  545.6 87.8 %reduce-scatter.8.cloned.1.call-start = ((), (), s32[]{:S(2)}) async-start(), calls=%async_computation.13 | async-start | bytes 2359296 | tf_op jit(solution)/shard_map/reduce_scatter | solution.py:320
  552.4 101.3 %reduce-scatter.4.cloned.1.call-start = ((), (), s32[]{:S(2)}) async-start(), calls=%async_computation.11 | async-start | bytes 1310720 | tf_op jit(solution)/shard_map/reduce_scatter | solution.py:320
  564.8 38.8 %collective-permute-start.52 = (bf16[128,2048]{1,0:T(8,128)(2,1)}, bf16[128,2048]{1,0:T(8,128)(2,1)S(1)}, u32[]{:S(2)}, u32[]{:S(2)}) collective-permute-start(bf16[128,2048]{1,0:T(8,128)(2,1)} %get-tuple-element.191), channel_id=1, source_target_pairs={{0,4},{4,0},{1,5},{5,1},{2,6},{6,2},{3,7},{7,3},{8,12},{12,8},{9,1... | collective-permute-start | bytes 1572872 | tf_op jit(solution)/shard_map/ppermute | solution.py:34
  564.9 38.7 %collective-permute-start.51 = (bf16[128,2048]{1,0:T(8,128)(2,1)}, bf16[128,2048]{1,0:T(8,128)(2,1)S(1)}, u32[]{:S(2)}, u32[]{:S(2)}) collective-permute-start(bf16[128,2048]{1,0:T(8,128)(2,1)} %get-tuple-element.189), channel_id=1, source_target_pairs={{0,1},{1,0},{2,3},{3,2},{4,5},{5,4},{6,7},{7,6},{8,9},{9,8},{10,11... | collective-permute-start | bytes 1572872 | tf_op jit(solution)/shard_map/ppermute | solution.py:33
  629.2 98.3 %all-to-all-start.5 = ((bf16[8,128,768]{2,1,0:T(8,128)(2,1)}), bf16[8,128,768]{2,1,0:T(8,128)(2,1)S(1)}, u32[]{:S(2)}, u32[]{:S(2)}) async-start(bf16[8,128,768]{2,1,0:T(8,128)(2,1)} %bitcast.173), calls=%async_computation.7 | async-start | bytes 3145728 | tf_op jit(solution)/shard_map/all_to_all | solution.py:312
  653.7 70.1 %collective-permute-start.55 = (bf16[128,1024]{1,0:T(8,128)(2,1)}, bf16[128,1024]{1,0:T(8,128)(2,1)S(1)}, u32[]{:S(2)}, u32[]{:S(2)}) collective-permute-start(bf16[128,1024]{1,0:T(8,128)(2,1)} %reduce-scatter.4.cloned.1.call-done), channel_id=1, source_target_pairs={{0,0},{8,1},{16,2},{24,3},{2,4},{10,5},{18,6},{26,7},{4,8},{12,9},... | collective-permute-start | bytes 786440 | tf_op jit(solution)/shard_map/ppermute | solution.py:324
  (96 other events, 1478.8 us)
Sparse Core Ops, SparseCore 0:
  32.3 105.8 all-gather.4
Sparse Core Ops, SparseCore 1:
  167.6 42.8 all-gather.8
  211.8 54.2 all-gather.6
  487.6 56.0 reduce-scatter.5
  552.5 64.4 reduce-scatter.7
  619.8 33.8 reduce-scatter.3

commit v3 on v2

--- a/solution.py
+++ b/solution.py
@@ -52,10 +52,10 @@
 
 def fold_cores(own, other):
     theirs = send_c(other)
+    rows = own.shape[0] // 4
     total = own + theirs.astype(f32)
-    rows = own.shape[0] // 4
-    part = [total[i * rows : (i + 1) * rows] for i in range(4)]
-    return part[0], [p.astype(bf16) for p in part[1:]]
+    low = [total[i * rows : (i + 1) * rows].astype(bf16) for i in range(1, 4)]
+    return total[:rows], low
 
 
 def finish(own, low):
@@ -191,12 +191,13 @@
     cos, sin, mask = tables
     rows, size = cos.shape[3], cos.shape[4]
     view = proj.reshape(2, 2, micro, rows, proj.shape[1])
+    width = (2 * group + 2) * size
     spec = functools.partial(rows_spec, rows)
     out = pl.pallas_call(
         functools.partial(forward_kernel, size, group),
         grid=(2, micro),
         in_specs=[
-            spec(proj.shape[1]),
+            spec(width),
             spec(size),
             spec(size),
             pl.BlockSpec((1, 1, 2 * rows, 2 * rows), lambda i, m: (i, m, 0, 0)),
@@ -212,12 +213,13 @@
 def attention_backward(proj, grad, tables, gains, group, micro):
     cos, sin, mask = tables
     rows, size = cos.shape[3], cos.shape[4]
+    width = (2 * group + 2) * size
     spec = functools.partial(rows_spec, rows)
     out, sums = pl.pallas_call(
         functools.partial(backward_kernel, size, group),
         grid=(2, micro),
         in_specs=[
-            spec(proj.shape[1]),
+            spec(width),
             spec(group * size),
             spec(size),
             spec(size),
@@ -225,11 +227,11 @@
             pl.BlockSpec((2, size), lambda i, m: (0, 0)),
         ],
         out_specs=[
-            spec(proj.shape[1]),
+            spec(width),
             pl.BlockSpec((1, 1, 2, size), lambda i, m: (i, m, 0, 0)),
         ],
         out_shape=[
-            jax.ShapeDtypeStruct((2, 2, micro, rows, proj.shape[1]), bf16),
+            jax.ShapeDtypeStruct((2, 2, micro, rows, width), bf16),
             jax.ShapeDtypeStruct((2, micro, 2, size), f32),
         ],
         name="attn_bwd",
@@ -241,7 +243,7 @@
         mask,
         gains,
     )
-    return out.reshape(proj.shape), jnp.sum(sums, axis=(0, 1))
+    return out.reshape(proj.shape[0], width), jnp.sum(sums, axis=(0, 1))
 
 
 def make_tables(lengths, side, rows, size):
@@ -283,29 +285,43 @@
     return out.reshape(copies * count, rows, width)
 
 
-def unpack_kernel(widths, got, *outs):
-    copies, count = got.shape[:2]
-    for i in range(count):
+def unpack_kernel(count, *refs):
+    got, *rest = refs
+    mats, outs, sums = rest[:count], rest[count:-1], rest[-1]
+    copies, pieces = got.shape[:2]
+    acc = jnp.zeros(sums.shape, f32)
+    for i in range(pieces):
         total = got[0, i].astype(f32)
         for j in range(1, copies):
             total = total + got[j, i].astype(f32)
         low = 0
-        for width, out in zip(widths, outs):
-            out[:, i * width : (i + 1) * width] = total[:, low : low + width]
+        for mat, out in zip(mats, outs):
+            width = out.shape[1] // pieces
+            part, place = total[:, low : low + width], slice(i * width, (i + 1) * width)
+            out[:, place] = part
+            part = part * mat[:, place].astype(f32)
+            for k in range(0, width, 128):
+                acc += part[:, k : k + 128]
             low += width
-
-
-def unpack_columns(got, count, widths):
-    copies, rows = got.shape[0] // count, got.shape[1]
+    sums[:, :] = acc
+
+
+def unpack_columns(got, count, mats):
+    copies, rows = got.shape[0] // count, mats[0].shape[0]
     step = min(rows, 32)
-    return pl.pallas_call(
-        functools.partial(unpack_kernel, widths),
+    specs = [pl.BlockSpec((step, m.shape[1]), lambda i: (i, 0)) for m in mats]
+    *outs, sums = pl.pallas_call(
+        functools.partial(unpack_kernel, len(mats)),
         grid=(rows // step,),
-        in_specs=[pl.BlockSpec((copies, count, step, got.shape[2]), lambda i: (0, 0, i, 0))],
-        out_specs=[pl.BlockSpec((step, count * w), lambda i: (i, 0)) for w in widths],
-        out_shape=[jax.ShapeDtypeStruct((rows, count * w), f32) for w in widths],
+        in_specs=[pl.BlockSpec((copies, count, step, got.shape[2]), lambda i: (0, 0, i, 0)), *specs],
+        out_specs=[*specs, pl.BlockSpec((step, 128), lambda i: (i, 0))],
+        out_shape=[
+            *(jax.ShapeDtypeStruct(m.shape, f32) for m in mats),
+            jax.ShapeDtypeStruct((rows, 128), f32),
+        ],
         name="unpack_columns",
-    )(got.reshape(copies, count, rows, got.shape[2]))
+    )(got.reshape(copies, count, *got.shape[1:]), *mats)
+    return *outs, jnp.sum(sums, axis=1)
 
 
 def exchange(blocks, axes):
@@ -346,13 +362,16 @@
     return full.reshape(count // col_count * rows, col_count * cols)
 
 
-def return_rows(grad, axes, route, col_count):
-    count = lax.axis_size(axes)
+def cut_rows(grad, count, col_count):
     rows, cols = grad.shape[0] // (count // col_count), grad.shape[1] // col_count
     blocks = [
         grad[i // col_count * rows :, i % col_count * cols :][:rows, :cols] for i in range(count)
     ]
-    mine = scatter(jnp.concatenate(blocks), axes, 0)
+    return jnp.concatenate(blocks)
+
+
+def return_rows(blocks, axes, route):
+    mine = scatter(blocks, axes, 0)
     return route_by(mine, [(b, a) for a, b in route]).astype(f32)
 
 
@@ -379,7 +398,7 @@
     micro, _, rows, width = block_input.shape
     size = gain_query.shape[0] * fsdp_count
     group = w_query.shape[1] // w_key.shape[1]
-    shards, near, wide = ("h", "g", "x", "c"), ("x", "c"), ("h", "x", "c")
+    shards, wide = ("h", "g", "x", "c"), ("h", "x", "c")
     plane_count = fsdp_count // 4
     route_out = row_route(4, fsdp_count, col_count)
     route_down = row_route(8, fsdp_count, col_count)
@@ -406,31 +425,21 @@
 
     tables = [make_tables(lengths_of(core), side, rows, size) for core in (0, 1)]
 
+    out_moved = route_by(w_out, route_out)
+    down_moved = route_by(w_down, route_down)
+    packed = pack_columns((w_query, w_key, w_value, w_gate_attn), 4, plane_count)
     packed_wide = pack_columns((w_gate, w_up), 8, 1)
-    packed = pack_columns((w_query, w_key, w_value, w_gate_attn), 4, 1)
-    moved = route_by(w_out, route_out)
-    spread = exchange(packed, near)
-    cut = moved.shape[1] // 4
-    moved = jnp.stack([moved[:, i * cut : (i + 1) * cut] for i in range(4)])
-    if moved.shape[1] == spread.shape[1]:
-        full = collect(jnp.concatenate([spread, moved], axis=2), data, 0)
-        full = full.reshape(plane_count, 4, *full.shape[1:])
-        qkvg, full = full[..., : spread.shape[2]], full[..., spread.shape[2] :]
-    else:
-        qkvg = collect(spread, data, 0)
-        full = collect(moved[None], data, 0)
-    qkvg = qkvg.reshape(width, spread.shape[2])
-    full = full.reshape(plane_count // col_count, col_count, 4, moved.shape[1], cut)
-    out_rows = full.transpose(0, 3, 1, 2, 4).reshape(-1, col_count * 4 * cut)
-    token_pair = gather_plane(after(tokens_low, spread), packed_wide)
-    cot_list = gather_plane(after(cotangent, token_pair[0]))
-    moved = route_by(after(w_down, token_pair[0]), route_down)
-    down_rows = join_rows(collect(moved[None], "g", 0), col_count)
-    far = send_mirror(after(cotangent, token_pair[0]))
-    cot_list += gather_plane(after(far, cot_list[0]))
-    spread = exchange(after(packed_wide, cot_list[0], far), wide)
+    qkvg = exchange(packed, shards)
+    qkvg = qkvg.reshape(width, qkvg.shape[2])
+    out_rows = join_rows(collect(out_moved[None], data, 0), col_count)
+    down_rows = join_rows(collect(down_moved[None], "g", 0), col_count)
+    token_pair = gather_plane(tokens_low, packed_wide)
+    spread = exchange(after(packed_wide, qkvg), wide)
     gate_up = collect(spread.reshape(2, -1, spread.shape[2]), "g", 1)
     gate_up = gate_up.reshape(-1, spread.shape[2])
+    cot_list = gather_plane(after(cotangent, token_pair[0]))
+    far = send_mirror(after(cotangent, qkvg))
+    cot_list += gather_plane(after(far, cot_list[0]))
 
     def first_norm(v):
         v = v.astype(f32)
@@ -488,28 +497,26 @@
     far_parts, near_parts = fold_cores(*far_parts), fold_cores(*near_parts)
     held = lax.optimization_barrier((*inner, *grad_units, *near_parts[1], *far_parts[1]))
     held_inner, held_units = held[:4], held[4:8]
+    sum_down = weight_grad(held_inner, cot_list)
+    sum_down = cut_rows(sum_down, plane_count // 2, col_count)
     sum_units = weight_grad(hidden_two, held_units)
     mine = scatter(sum_units.reshape(2, width // 2, 2 * units), "g", 1)
     final_parts = products(held_inner, down_rows, 0)
     held = lax.optimization_barrier((*final_parts[0], *final_parts[1]))
     final_parts = fold_cores(*held[:2]), fold_cores(*held[2:])
-    sum_down = weight_grad(held_inner, cot_list)
     grad_hidden_two = after(finish_pair(near_parts, far_parts), sum_down, sum_units)
 
-    back, addend = norm_back(grad_hidden_two, residual, scale_two, gain_two)
-    sum_two = jnp.sum(addend, axis=0)
+    back, _ = norm_back(grad_hidden_two, residual, scale_two, gain_two)
     grad_resid = cotangent.astype(f32) + back
-    low = grad_resid.astype(bf16)
-    low_pair = gather_plane(low)
+    low_pair = gather_plane(grad_resid.astype(bf16), *final_parts[0][1], *final_parts[1][1])
     got = exchange(mine.reshape(8, mine.shape[1] // 4, mine.shape[2]), wide)
-    grad_gate, grad_up = unpack_columns(got, 8, (units, units))
-    grad_down = return_rows(sum_down, "g", route_down, col_count)
-    sum_out = weight_grad(gated, low_pair)
-    grad_out = return_rows(sum_out, data, route_out, col_count)
-    held = lax.optimization_barrier((*low_pair, sum_out))[:2]
+    grad_gate, grad_up, sum_two = unpack_columns(got, 8, (w_gate, w_up))
+    grad_down = return_rows(sum_down, "g", route_down)
+    sum_out = cut_rows(weight_grad(gated, low_pair), plane_count, col_count)
+    grad_out = return_rows(sum_out, data, route_out)
     final = finish_pair(*final_parts)
-    block_output = (residual + final).astype(bf16).reshape(block_input.shape)
-    grad_gated = [dot(d, out_rows, 1, 1) for d in held]
+    block_output = (after(residual, low_pair[0]) + final).astype(bf16).reshape(block_input.shape)
+    grad_gated = [dot(low_pair[0], out_rows, 1, 1), dot(after(low_pair[1], sum_out), out_rows, 1, 1)]
 
     def attention_part(i):
         return attention_backward(proj[i], grad_gated[i], tables[i], head_gains, group, micro)
@@ -517,41 +524,35 @@
     backs = [attention_part(0), attention_part(1)]
     grad_proj = [b[0] for b in backs]
     sum_proj = weight_grad(hidden, grad_proj)
-    got = exchange(sum_proj.reshape(fsdp_count, -1, sum_proj.shape[1]), shards)
-    query_width, key_width = group * size, size
-    grad_query, grad_key, grad_value, grad_gate_attn = unpack_columns(
-        got, 4, (query_width, key_width, key_width, query_width)
-    )
+    head_sums = (backs[0][1] + backs[1][1]).astype(bf16).reshape(1, 1, 2 * size)
+    tail = jnp.pad(head_sums, ((0, 0), (0, 7), (0, sum_proj.shape[1] - 2 * size)))
+    tail = jnp.broadcast_to(tail, (fsdp_count, *tail.shape[1:]))
+    tail = jnp.concatenate([sum_proj.reshape(fsdp_count, -1, sum_proj.shape[1]), tail], axis=1)
+    got = exchange(tail, shards)
+    mats = (w_query, w_key, w_value, w_gate_attn)
+    grad_query, grad_key, grad_value, grad_gate_attn, sum_one = unpack_columns(got, 4, mats)
+    head_sums = jnp.sum(got[:, w_query.shape[0], : 2 * size].astype(f32), axis=0)
     grad_proj = lax.optimization_barrier((*grad_proj, sum_proj, block_output))[:2]
     parts = dot(grad_proj[0], qkvg, 1, 1), dot(grad_proj[1], qkvg, 1, 1, bf16)
     grad_hidden = finish(*fold_cores(*parts))
-    back, addend = norm_back(grad_hidden, tokens, rms_scale(tokens), gain_one)
+    back, _ = norm_back(grad_hidden, tokens, rms_scale(tokens), gain_one)
     grad_input = (grad_resid + back).reshape(block_input.shape)
 
-    head_sums = backs[0][1] + backs[1][1]
-    sums = jnp.concatenate(
-        [
-            jnp.sum(addend, axis=0).reshape(fsdp_count, piece),
-            sum_two.reshape(fsdp_count, piece),
-            head_sums[0].reshape(fsdp_count, small),
-            head_sums[1].reshape(fsdp_count, small),
-        ],
-        axis=1,
-    )
-    mine = jnp.sum(exchange(after(sums, got), shards), axis=0)
+    mine = jnp.concatenate([sum_one, sum_two, head_sums])
     mine = mine + lax.ppermute(mine, "y", swap)
+    head_sums = lax.dynamic_slice_in_dim(mine[2 * piece :].reshape(2, size), owner * small, small, 1)
     return (
         block_output,
         grad_input,
-        mine[:piece],
+        mine[:piece] / norm_attn.astype(f32),
         grad_query,
         grad_key,
         grad_value,
         grad_gate_attn,
         grad_out,
-        mine[2 * piece : 2 * piece + small],
-        mine[2 * piece + small :],
-        mine[piece : 2 * piece],
+        head_sums[0],
+        head_sums[1],
+        mine[piece : 2 * piece] / norm_ffn.astype(f32),
         grad_gate,
         grad_up,
         grad_down,

time: 756 us -> 742 us (0.981)
  waiting for transfers between devices: 345 us -> 325 us
  other arithmetic: 44.1 us -> 60 us
  starting transfers between devices: 130 us -> 121 us
    ppermute x12, waiting for transfers between devices: 84 us -> 111 us  [send_plane(): lax.ppermute(xy, ('x', 'y'), cross)]
    all_to_all x6 -> x5, waiting for transfers between devices: 35.2 us -> 9.03 us  [exchange(): return lax.all_to_all(blocks, axes, split_axis=0, concat_axis=0, tiled=True)]
    ppermute x4, waiting for transfers between devices: 74 us -> 50.3 us  [route_by(): return lax.ppermute(v, every, pairs)]
    ppermute x12, starting transfers between devices: 13.1 us -> 28.1 us  [send_c(): return lax.ppermute(v, 'c', swap)]
    all_to_all x6 -> x5, starting transfers between devices: 41.4 us -> 26.9 us  [exchange(): return lax.all_to_all(blocks, axes, split_axis=0, concat_axis=0, tiled=True)]
    reduce_scatter x3, waiting for transfers between devices: 12.7 us -> 0.03 us  [scatter(): return lax.psum_scatter(full, axes, scatter_dimension=axis, tiled=True)]
    ppermute x12, waiting for transfers between devices: 57 us -> 69 us  [send_plane(): lax.ppermute(x, 'x', swap)]
    unnamed x117 -> x121, local copies, waits for them, and re-layouts: 19.9 us -> 18.1 us
  transfers between devices with their start and end apart: 69 -> 68, of which waited for: 31 -> 27; matrix products, arithmetic and copies ran while one was open for 26% -> 27% of each run, Pallas kernels for 5% -> 5%
where the time goes in v3:
time: 742 us; the launch traced here: 732 us
  waiting for transfers between devices  325 us (44%)
  matrix products  128 us (17%)
  starting transfers between devices  121 us (16%)
  other arithmetic  60 us (8%)
  Pallas kernels  43.7 us (6%)
  local copies, waits for them, and re-layouts  37.7 us (5%)
  between operations  17 us (2%)
    dot_general x36, matrix products, dot(): lax.dot_general(a, b, (((ca,), (cb,)), ((), ())), preferred_element_type=...  128 us
    ppermute x12, waiting for transfers between devices, send_plane(): lax.ppermute(xy, ('x', 'y'), cross)  111 us
    ppermute x12, waiting for transfers between devices, send_plane(): lax.ppermute(x, 'x', swap)  69 us
    ppermute x4, waiting for transfers between devices, route_by(): return lax.ppermute(v, every, pairs)  50.3 us
    all_gather x3, waiting for transfers between devices, collect(): return lax.all_gather(mine, axes, axis=axis, tiled=True)  36.8 us
    ppermute x12, starting transfers between devices, send_c(): return lax.ppermute(v, 'c', swap)  28.1 us
    all_to_all x5, starting transfers between devices, exchange(): return lax.all_to_all(blocks, axes, split_axis=0, concat_axis=0, tiled=True)  26.9 us
    ppermute x12, waiting for transfers between devices, send_plane(): lax.ppermute(y, 'y', swap)  26.8 us
  transfers between devices with their start and end apart: 68, of which 27 were waited for; matrix products, arithmetic and copies ran while one was open for 27% of the time, Pallas kernels for 5%

profile of v3, /device:TPU:1, one launch (start us, length us, event | category | flops | bytes accessed | tf_op | source)
XLA Modules:
  0.0 731.9 jit_solution(5405163245912943420)
XLA Ops:
  13.5 7.3 all-to-all-start
  42.6 28.9 %collective-permute-done.2 = bf16[128,2048]{1,0:T(8,128)(2,1)S(1)} collective-permute-done((bf16[128,2048]{1,0:T(8,128)(2,1)S(1)}, bf16[128,2048]{1,0:T(8,128)(2,1)S(1)}, u32[]{:S(2)}, u32[]{:S(2)}) %collective-permute-start.2) | collective-permute-done | bytes 524320 | tf_op jit(solution)/shard_map/ppermute | solution.py:35
  71.5 15.4 %collective-permute-done.1 = bf16[128,2048]{1,0:T(8,128)(2,1)S(1)} collective-permute-done((bf16[128,2048]{1,0:T(8,128)(2,1)S(1)}, bf16[128,2048]{1,0:T(8,128)(2,1)S(1)}, u32[]{:S(2)}, u32[]{:S(2)}) %collective-permute-start.1) | collective-permute-done | bytes 524320 | tf_op jit(solution)/shard_map/ppermute | solution.py:34
  101.3 36.8 %all-gather.8.cloned.1.call-done = bf16[512,1024]{1,0:T(8,128)(2,1)} async-done(((bf16[128,1024]{1,0:T(8,128)(2,1)}), bf16[512,1024]{1,0:T(8,128)(2,1)}) %all-gather.8.cloned.1.call-update) | async-done | bytes 1048592 | tf_op jit(solution)/shard_map/all_gather | solution.py:332
  161.8 7.4 %collective-permute-start.12 = (bf16[384,1024]{1,0:T(8,128)(2,1)}, bf16[384,1024]{1,0:T(8,128)(2,1)}, u32[]{:S(2)}, u32[]{:S(2)}) collective-permute-start(bf16[384,1024]{1,0:T(8,128)(2,1)} %param.28), channel_id=1, source_target_pairs={{0,0},{1,8},{2,2},{3,10},{4,4},{5,12},{6,6},{7,14},{8,16},{9,24},{... | collective-permute-start | bytes 2359304 | tf_op jit(solution)/shard_map/ppermute | solution.py:340
  197.8 18.9 %collective-permute-done.8 = bf16[128,2048]{1,0:T(8,128)(2,1)S(1)} collective-permute-done((bf16[128,2048]{1,0:T(8,128)(2,1)}, bf16[128,2048]{1,0:T(8,128)(2,1)S(1)}, u32[]{:S(2)}, u32[]{:S(2)}) %collective-permute-start.8) | collective-permute-done | bytes 524320 | tf_op jit(solution)/shard_map/ppermute | solution.py:35
  216.7 10.1 %collective-permute-done.7 = bf16[128,2048]{1,0:T(8,128)(2,1)S(1)} collective-permute-done((bf16[128,2048]{1,0:T(8,128)(2,1)}, bf16[128,2048]{1,0:T(8,128)(2,1)S(1)}, u32[]{:S(2)}, u32[]{:S(2)}) %collective-permute-start.7) | collective-permute-done | bytes 524320 | tf_op jit(solution)/shard_map/ppermute | solution.py:34
  242.9 7.6 %collective-permute-done.15 = bf16[128,2048]{1,0:T(8,128)(2,1)S(1)} collective-permute-done((bf16[128,2048]{1,0:T(8,128)(2,1)S(1)}, bf16[128,2048]{1,0:T(8,128)(2,1)S(1)}, u32[]{:S(2)}, u32[]{:S(2)}) %collective-permute-start.15) | collective-permute-done | bytes 524320 | tf_op jit(solution)/shard_map/ppermute | solution.py:35
  254.0 6.6 collective-permute-done.14
  265.1 7.9 %collective-permute-done.11 = bf16[128,2048]{1,0:T(8,128)(2,1)S(1)} collective-permute-done((bf16[128,2048]{1,0:T(8,128)(2,1)S(1)}, bf16[128,2048]{1,0:T(8,128)(2,1)S(1)}, u32[]{:S(2)}, u32[]{:S(2)}) %collective-permute-start.11) | collective-permute-done | bytes 524320 | tf_op jit(solution)/shard_map/ppermute | solution.py:35
  288.6 9.3 %collective-permute-done.29 = bf16[128,2048]{1,0:T(8,128)(2,1)S(1)} collective-permute-done((bf16[128,2048]{1,0:T(8,128)(2,1)}, bf16[128,2048]{1,0:T(8,128)(2,1)S(1)}, u32[]{:S(2)}, u32[]{:S(2)}) %collective-permute-start.29) | collective-permute-done | bytes 524320 | tf_op jit(solution)/shard_map/ppermute | solution.py:35
  302.4 12.9 %collective-permute-start.31 = (bf16[512,2048]{1,0:T(8,128)(2,1)}, bf16[512,2048]{1,0:T(8,128)(2,1)}, u32[]{:S(2)}, u32[]{:S(2)}) collective-permute-start(bf16[512,2048]{1,0:T(8,128)(2,1)} %constant_dynamic-update-slice_fusion.8), channel_id=1, source_target_pairs={{0,2},{2,0},{1,3},{3,1},{4,6},{6,4},{5,7},{7,5},{8,10},{10,8},{9,1... | collective-permute-start | bytes 6291464 | tf_op jit(solution)/shard_map/ppermute | solution.py:28
  321.2 7.2 collective-permute-start.30
  424.1 20.1 %collective-permute-done.36 = bf16[128,2048]{1,0:T(8,128)(2,1)} collective-permute-done((bf16[128,2048]{1,0:T(8,128)(2,1)S(1)}, bf16[128,2048]{1,0:T(8,128)(2,1)}, u32[]{:S(2)}, u32[]{:S(2)}) %collective-permute-start.36) | collective-permute-done | bytes 524320 | tf_op jit(solution)/shard_map/ppermute | solution.py:41
  451.2 11.2 %collective-permute-done.39 = bf16[128,2048]{1,0:T(8,128)(2,1)S(1)} collective-permute-done((bf16[128,2048]{1,0:T(8,128)(2,1)S(1)}, bf16[128,2048]{1,0:T(8,128)(2,1)S(1)}, u32[]{:S(2)}, u32[]{:S(2)}) %collective-permute-start.39) | collective-permute-done | bytes 524320 | tf_op jit(solution)/shard_map/ppermute | solution.py:35
  462.4 11.1 %collective-permute-done.38 = bf16[128,2048]{1,0:T(8,128)(2,1)S(1)} collective-permute-done((bf16[128,2048]{1,0:T(8,128)(2,1)S(1)}, bf16[128,2048]{1,0:T(8,128)(2,1)S(1)}, u32[]{:S(2)}, u32[]{:S(2)}) %collective-permute-start.38) | collective-permute-done | bytes 524320 | tf_op jit(solution)/shard_map/ppermute | solution.py:34
  490.7 8.9 %attn_bwd.2 = (bf16[2,2,2,64,768]{4,3,2,1,0:T(8,128)(2,1)}, f32[2,2,2,128]{3,2,1,0:T(2,128)}) custom-call(f32[2,2,2,64,768]{4,3,2,1,0:T(8,128)} %fusion.69.proj, f32[2,2,2,64,256]{4,3,2,1,0:T(8,128)} %fusion.33.grad, f32[2,2,2,64,128]{4,3,2,1,0:T(8,128)} %maximum_bitcast_fusion.2.cos, f32[2,2,2,64,128]{4,3,2,1,0:T(8,128)} %maximum_bitcast_fusion.3.sin, ...), custom_call_target="tpu_custom_call" | custom-call | tf_op jit(solution)/shard_map/attn_bwd/pallas_call | solution.py:218
  518.4 9.0 %attn_bwd.3 = (bf16[2,2,2,64,768]{4,3,2,1,0:T(8,128)(2,1)}, f32[2,2,2,128]{3,2,1,0:T(2,128)}) custom-call(f32[2,2,2,64,768]{4,3,2,1,0:T(8,128)} %fusion.68.proj, f32[2,2,2,64,256]{4,3,2,1,0:T(8,128)} %fusion.31.grad, f32[2,2,2,64,128]{4,3,2,1,0:T(8,128)} %maximum_bitcast_fusion.cos, f32[2,2,2,64,128]{4,3,2,1,0:T(8,128)} %maximum_bitcast_fusion.1.sin, ...), custom_call_target="tpu_custom_call" | custom-call | tf_op jit(solution)/shard_map/attn_bwd/pallas_call | solution.py:218
  535.1 6.6 all-to-all-done.4
  557.4 24.2 %collective-permute-done.47 = bf16[128,2048]{1,0:T(8,128)(2,1)} collective-permute-done((bf16[128,2048]{1,0:T(8,128)(2,1)S(1)}, bf16[128,2048]{1,0:T(8,128)(2,1)}, u32[]{:S(2)}, u32[]{:S(2)}) %collective-permute-start.47) | collective-permute-done | bytes 524320 | tf_op jit(solution)/shard_map/ppermute | solution.py:35
  581.6 16.9 %collective-permute-done.46 = bf16[128,2048]{1,0:T(8,128)(2,1)} collective-permute-done((bf16[128,2048]{1,0:T(8,128)(2,1)}, bf16[128,2048]{1,0:T(8,128)(2,1)}, u32[]{:S(2)}, u32[]{:S(2)}) %collective-permute-start.46) | collective-permute-done | bytes 524320 | tf_op jit(solution)/shard_map/ppermute | solution.py:34
  605.2 7.4 %collective-permute-start.56 = (bf16[384,1024]{1,0:T(8,128)(2,1)}, bf16[384,1024]{1,0:T(8,128)(2,1)}, u32[]{:S(2)}, u32[]{:S(2)}) collective-permute-start(bf16[384,1024]{1,0:T(8,128)(2,1)} %reduce-scatter.8.cloned.1.call-done), channel_id=1, source_target_pairs={{0,0},{8,1},{2,2},{10,3},{4,4},{12,5},{6,6},{14,7},{16,8},{24,9},{... | collective-permute-start | bytes 2359304 | tf_op jit(solution)/shard_map/ppermute | solution.py:340
  626.7 21.8 %collective-permute-done.41 = bf16[128,2048]{1,0:T(8,128)(2,1)} collective-permute-done((bf16[128,2048]{1,0:T(8,128)(2,1)}, bf16[128,2048]{1,0:T(8,128)(2,1)}, u32[]{:S(2)}, u32[]{:S(2)}) %collective-permute-start.41) | collective-permute-done | bytes 524320 | tf_op jit(solution)/shard_map/ppermute | solution.py:33
  658.4 47.9 %collective-permute-done.55 = bf16[128,1024]{1,0:T(8,128)(2,1)S(1)} collective-permute-done((bf16[128,1024]{1,0:T(8,128)(2,1)}, bf16[128,1024]{1,0:T(8,128)(2,1)S(1)}, u32[]{:S(2)}, u32[]{:S(2)}) %collective-permute-start.55) | collective-permute-done | bytes 262176 | tf_op jit(solution)/shard_map/ppermute | solution.py:340
  (383 shorter events, 353.5 us)
Async XLA Ops:
  26.7 119.6 %all-to-all-start.1 = ((bf16[16,128,768]{2,1,0:T(8,128)(2,1)}), bf16[16,128,768]{2,1,0:T(8,128)(2,1)}, u32[]{:S(2)}, u32[]{:S(2)}) async-start(bf16[16,128,768]{2,1,0:T(8,128)(2,1)} %bitcast.153), calls=%async_computation.1 | async-start | bytes 6291456 | tf_op jit(solution)/shard_map/all_to_all | solution.py:328
  31.8 106.3 %all-gather.8.cloned.1.call-start = ((), (), s32[]{:S(2)}) async-start(), calls=%async_computation.12 | async-start | bytes 1310720 | tf_op jit(solution)/shard_map/all_gather | solution.py:332
  34.2 52.7 %collective-permute-start.1 = (bf16[128,2048]{1,0:T(8,128)(2,1)S(1)}, bf16[128,2048]{1,0:T(8,128)(2,1)S(1)}, u32[]{:S(2)}, u32[]{:S(2)}) collective-permute-start(bf16[128,2048]{1,0:T(8,128)(2,1)S(1)} %bitcast.149), channel_id=1, source_target_pairs={{0,4},{4,0},{1,5},{5,1},{2,6},{6,2},{3,7},{7,3},{8,12},{12,8},{9,1... | collective-permute-start | bytes 1572872 | tf_op jit(solution)/shard_map/ppermute | solution.py:34
  34.3 53.4 %collective-permute-start = (bf16[128,2048]{1,0:T(8,128)(2,1)S(1)}, bf16[128,2048]{1,0:T(8,128)(2,1)}, u32[]{:S(2)}, u32[]{:S(2)}) collective-permute-start(bf16[128,2048]{1,0:T(8,128)(2,1)S(1)} %bitcast.150), channel_id=1, source_target_pairs={{0,1},{1,0},{2,3},{3,2},{4,5},{5,4},{6,7},{7,6},{8,9},{9,8},{10,11... | collective-permute-start | bytes 1572872 | tf_op jit(solution)/shard_map/ppermute | solution.py:33
  34.6 58.4 %collective-permute-start.4 = (bf16[128,1024]{1,0:T(8,128)(2,1)}, bf16[128,1024]{1,0:T(8,128)(2,1)S(1)}, u32[]{:S(2)}, u32[]{:S(2)}) collective-permute-start(bf16[128,1024]{1,0:T(8,128)(2,1)} %param.22), channel_id=1, source_target_pairs={{0,0},{1,8},{2,16},{3,24},{4,2},{5,10},{6,18},{7,26},{8,4},{9,12},... | collective-permute-start | bytes 786440 | tf_op jit(solution)/shard_map/ppermute | solution.py:340
  170.9 61.4 %all-to-all-start.2 = ((bf16[8,128,768]{2,1,0:T(8,128)(2,1)}), bf16[8,128,768]{2,1,0:T(8,128)(2,1)}, u32[]{:S(2)}, u32[]{:S(2)}) async-start(bf16[8,128,768]{2,1,0:T(8,128)(2,1)} %bitcast.159), calls=%async_computation.2 | async-start | bytes 3145728 | tf_op jit(solution)/shard_map/all_to_all | solution.py:328
  175.1 99.6 %all-gather.10.cloned.1.call-start = ((), (), s32[]{:S(2)}) async-start(), calls=%async_computation.13 | async-start | bytes 2359296 | tf_op jit(solution)/shard_map/all_gather | solution.py:332
  196.3 132.0 %all-gather.6.cloned.1.call-start = ((), (), s32[]{:S(2)}) async-start(), calls=%async_computation.8 | async-start | bytes 4718592 | tf_op jit(solution)/shard_map/all_gather | solution.py:332
  232.3 267.3 %reduce-scatter.4.cloned.1.call-start = ((), (), s32[]{:S(2)}) async-start(), calls=%async_computation.9 | async-start | bytes 4718592 | tf_op jit(solution)/shard_map/reduce_scatter | solution.py:336
  262.3 66.0 %collective-permute-start.17 = (bf16[512,2048]{1,0:T(8,128)(2,1)}, bf16[512,2048]{1,0:T(8,128)(2,1)}, u32[]{:S(2)}, u32[]{:S(2)}) collective-permute-start(bf16[512,2048]{1,0:T(8,128)(2,1)} %pad_maximum_fusion.2), channel_id=1, source_target_pairs={{0,2},{2,0},{1,3},{3,1},{4,6},{6,4},{5,7},{7,5},{8,10},{10,8},{9,1... | collective-permute-start | bytes 6291464 | tf_op jit(solution)/shard_map/ppermute | solution.py:28
  273.8 58.8 %collective-permute-start.16 = (bf16[512,2048]{1,0:T(8,128)(2,1)}, bf16[512,2048]{1,0:T(8,128)(2,1)}, u32[]{:S(2)}, u32[]{:S(2)}) collective-permute-start(bf16[512,2048]{1,0:T(8,128)(2,1)} %constant_dynamic-update-slice_fusion), channel_id=1, source_target_pairs={{0,2},{2,0},{1,3},{3,1},{4,6},{6,4},{5,7},{7,5},{8,10},{10,8},{9,1... | collective-permute-start | bytes 6291464 | tf_op jit(solution)/shard_map/ppermute | solution.py:28
  370.7 53.0 %collective-permute-start.21 = (bf16[128,2048]{1,0:T(8,128)(2,1)}, bf16[128,2048]{1,0:T(8,128)(2,1)}, u32[]{:S(2)}, u32[]{:S(2)}) collective-permute-start(bf16[128,2048]{1,0:T(8,128)(2,1)} %get-tuple-element.194), channel_id=1, source_target_pairs={{0,5},{5,0},{1,4},{4,1},{2,7},{7,2},{3,6},{6,3},{8,13},{13,8},{9,1... | collective-permute-start | bytes 1572872 | tf_op jit(solution)/shard_map/ppermute | solution.py:35
  371.6 52.5 %collective-permute-start.20 = (bf16[128,2048]{1,0:T(8,128)(2,1)}, bf16[128,2048]{1,0:T(8,128)(2,1)}, u32[]{:S(2)}, u32[]{:S(2)}) collective-permute-start(bf16[128,2048]{1,0:T(8,128)(2,1)} %get-tuple-element.195), channel_id=1, source_target_pairs={{0,4},{4,0},{1,5},{5,1},{2,6},{6,2},{3,7},{7,3},{8,12},{12,8},{9,1... | collective-permute-start | bytes 1572872 | tf_op jit(solution)/shard_map/ppermute | solution.py:34
  407.9 197.3 %reduce-scatter.8.cloned.1.call-start = ((), (), s32[]{:S(2)}) async-start(), calls=%async_computation.11 | async-start | bytes 2359296 | tf_op jit(solution)/shard_map/reduce_scatter | solution.py:336
  412.9 67.3 %collective-permute-start.40 = (bf16[512,2048]{1,0:T(8,128)(2,1)}, bf16[512,2048]{1,0:T(8,128)(2,1)}, u32[]{:S(2)}, u32[]{:S(2)}) collective-permute-start(bf16[512,2048]{1,0:T(8,128)(2,1)} %convolution_convert_fusion.3), channel_id=1, source_target_pairs={{0,2},{2,0},{1,3},{3,1},{4,6},{6,4},{5,7},{7,5},{8,10},{10,8},{9,1... | collective-permute-start | bytes 6291464 | tf_op jit(solution)/shard_map/ppermute | solution.py:28
  423.7 52.3 %collective-permute-start.44 = (bf16[512,2048]{1,0:T(8,128)(2,1)}, bf16[512,2048]{1,0:T(8,128)(2,1)S(1)}, u32[]{:S(2)}, u32[]{:S(2)}) collective-permute-start(bf16[512,2048]{1,0:T(8,128)(2,1)} %convolution_convert_fusion.2), channel_id=1, source_target_pairs={{0,2},{2,0},{1,3},{3,1},{4,6},{6,4},{5,7},{7,5},{8,10},{10,8},{9,1... | collective-permute-start | bytes 6291464 | tf_op jit(solution)/shard_map/ppermute | solution.py:28
  541.7 172.4 %all-to-all-start.3 = ((bf16[16,136,768]{2,1,0:T(8,128)(2,1)}), bf16[16,136,768]{2,1,0:T(8,128)(2,1)}, u32[]{:S(2)}, u32[]{:S(2)}) async-start(bf16[16,136,768]{2,1,0:T(8,128)(2,1)} %pad_maximum_fusion), calls=%async_computation.3 | async-start | bytes 6684672 | tf_op jit(solution)/shard_map/all_to_all | solution.py:328
  546.8 103.9 %reduce-scatter.6.cloned.1.call-start = ((), (), s32[]{:S(2)}) async-start(), calls=%async_computation.10 | async-start | bytes 1310720 | tf_op jit(solution)/shard_map/reduce_scatter | solution.py:336
  552.0 53.2 %collective-permute-start.50 = (bf16[512,2048]{1,0:T(8,128)(2,1)}, bf16[512,2048]{1,0:T(8,128)(2,1)}, u32[]{:S(2)}, u32[]{:S(2)}) collective-permute-start(bf16[512,2048]{1,0:T(8,128)(2,1)} %convolution_convert_fusion.1), channel_id=1, source_target_pairs={{0,2},{2,0},{1,3},{3,1},{4,6},{6,4},{5,7},{7,5},{8,10},{10,8},{9,1... | collective-permute-start | bytes 6291464 | tf_op jit(solution)/shard_map/ppermute | solution.py:28
  555.3 65.0 %collective-permute-start.43 = (bf16[128,2048]{1,0:T(8,128)(2,1)}, bf16[128,2048]{1,0:T(8,128)(2,1)S(1)}, u32[]{:S(2)}, u32[]{:S(2)}) collective-permute-start(bf16[128,2048]{1,0:T(8,128)(2,1)} %get-tuple-element.188), channel_id=1, source_target_pairs={{0,5},{5,0},{1,4},{4,1},{2,7},{7,2},{3,6},{6,3},{8,13},{13,8},{9,1... | collective-permute-start | bytes 1572872 | tf_op jit(solution)/shard_map/ppermute | solution.py:35
  620.3 86.9 %collective-permute-start.53 = (bf16[128,2048]{1,0:T(8,128)(2,1)}, bf16[128,2048]{1,0:T(8,128)(2,1)S(1)}, u32[]{:S(2)}, u32[]{:S(2)}) collective-permute-start(bf16[128,2048]{1,0:T(8,128)(2,1)} %get-tuple-element.185), channel_id=1, source_target_pairs={{0,5},{5,0},{1,4},{4,1},{2,7},{7,2},{3,6},{6,3},{8,13},{13,8},{9,1... | collective-permute-start | bytes 1572872 | tf_op jit(solution)/shard_map/ppermute | solution.py:35
  626.7 80.5 %collective-permute-start.52 = (bf16[128,2048]{1,0:T(8,128)(2,1)}, bf16[128,2048]{1,0:T(8,128)(2,1)S(1)}, u32[]{:S(2)}, u32[]{:S(2)}) collective-permute-start(bf16[128,2048]{1,0:T(8,128)(2,1)} %get-tuple-element.186), channel_id=1, source_target_pairs={{0,4},{4,0},{1,5},{5,1},{2,6},{6,2},{3,7},{7,3},{8,12},{12,8},{9,1... | collective-permute-start | bytes 1572872 | tf_op jit(solution)/shard_map/ppermute | solution.py:34
  648.5 58.7 %collective-permute-start.51 = (bf16[128,2048]{1,0:T(8,128)(2,1)}, bf16[128,2048]{1,0:T(8,128)(2,1)S(1)}, u32[]{:S(2)}, u32[]{:S(2)}) collective-permute-start(bf16[128,2048]{1,0:T(8,128)(2,1)} %get-tuple-element.184), channel_id=1, source_target_pairs={{0,1},{1,0},{2,3},{3,2},{4,5},{5,4},{6,7},{7,6},{8,9},{9,8},{10,11... | collective-permute-start | bytes 1572872 | tf_op jit(solution)/shard_map/ppermute | solution.py:33
  650.7 55.6 %collective-permute-start.55 = (bf16[128,1024]{1,0:T(8,128)(2,1)}, bf16[128,1024]{1,0:T(8,128)(2,1)S(1)}, u32[]{:S(2)}, u32[]{:S(2)}) collective-permute-start(bf16[128,1024]{1,0:T(8,128)(2,1)} %reduce-scatter.6.cloned.1.call-done), channel_id=1, source_target_pairs={{0,0},{8,1},{16,2},{24,3},{2,4},{10,5},{18,6},{26,7},{4,8},{12,9},... | collective-permute-start | bytes 786440 | tf_op jit(solution)/shard_map/ppermute | solution.py:340
  (98 other events, 1804.1 us)
Sparse Core Ops, SparseCore 0:
  93.8 44.2 all-gather.7
Sparse Core Ops, SparseCore 1:
  196.4 39.5 all-gather.9
  237.4 61.5 all-gather.5
  408.0 55.9 reduce-scatter.3
  487.3 31.2 reduce-scatter.7
  555.1 52.9 reduce-scatter.5
